TPU v7x, 128 devices: a whole 4x4x4 slice. The times are simulated.
128 devices in a mesh: front: 4 (over z_lo, core), grid: 32 (over z_hi, y, x).
Axes of the slice: x: 4, y: 4, z: 4 (z_hi: 2, z_lo: 2; z = z_hi * 2 + z_lo), core: 2. Of those that a mesh axis runs over, the one named last changes fastest.
Arguments:
- index_map: int32 [4, 8192], P('front'), may hold values from 0 to 16383, as said below
- lengths: int32 [4], P('front'), may hold values from 1 to 8192, 24576 in all
- update_front: float32 [4, 8192, 8192], P('front', 'grid'), may hold values from -0.0625 to 0.0625
- front_matrix: float32 [16384, 16384], P(('front', 'grid')), may hold values from -0.046875 to 0.046875
- random: float32 [16384, 256], P(('front', 'grid')), may hold values from -6 to 6
Outputs:
- parent_sample: float32 [16384, 256], P(('front', 'grid'))
Inputs may be any that keep to these rules, and one draw needn't show every extreme that they name: `index_map`: within one child the 8192 entries are distinct parent rows. `lengths`: rows of a child at or past its length are not live; the largest length equals 8192.
All inputs are finite; a program needn't handle non-finite values. No bound on the sum of `lengths` on one device may be relied on, other than what follows from the above.
Results may differ from a plain program's by a relative error of at most 0.0003.
Values sent between devices are 32-bit elements; how exact they have to be, the bound alone decides.
No kernel may reach another device: no remote copies, remote signals or barrier semaphores. Data moves between devices by JAX's collectives and lax.ppermute only.
A program may use at most 128 MiB of HBM per device.

v0:
```python
import jax
import jax.numpy as jnp
from jax import lax
from jax.sharding import PartitionSpec as P


def split_up(array, dim, length):
    shape = array.shape
    blocks = array.reshape(*shape[:dim], length, shape[dim] // length, *shape[dim + 1 :])
    return jnp.moveaxis(blocks, dim, 0)


def sum_at_owner(array, axis, dim):
    length = lax.axis_size(axis)
    blocks = lax.all_to_all(split_up(array, dim, length), axis, 0, 0, tiled=True)
    return jnp.sum(blocks, axis=0)


def shards(index_map, lengths, update_front, front_matrix, random):
    gathered_random = lax.all_gather(random, ("front", "grid"), axis=0, tiled=True)
    parent_part = jnp.dot(
        front_matrix,
        gathered_random,
        preferred_element_type=jnp.float32,
        precision=lax.Precision.HIGHEST,
    )
    index_rows = index_map[0]
    child_random = jnp.take(gathered_random, index_rows, axis=0)
    child_sample = jnp.dot(
        update_front[0],
        child_random,
        preferred_element_type=jnp.float32,
        precision=lax.Precision.HIGHEST,
    )
    local_rows = child_sample.shape[0]
    first_row = lax.axis_index("grid") * local_rows
    row_numbers = first_row + jnp.arange(local_rows, dtype=jnp.int32)
    live_rows = row_numbers < lengths[0]
    child_sample = jnp.where(live_rows[:, None], child_sample, jnp.float32(0.0))
    own_rows = parent_part.shape[0]
    group_sample = lax.all_gather(child_sample, "grid", axis=0, tiled=True)
    group_count = lax.axis_size("front")
    grid_count = lax.axis_size("grid")
    grid_place = lax.axis_index("grid")
    block_ids = jnp.arange(group_count, dtype=jnp.int32)[:, None] * grid_count + grid_place
    targets = (block_ids * own_rows + jnp.arange(own_rows, dtype=jnp.int32)[None, :]).reshape(-1)
    one_hot = (targets[:, None] == index_rows[None, :]).astype(jnp.float32)
    terms = jnp.dot(
        one_hot, group_sample, preferred_element_type=jnp.float32, precision=lax.Precision.HIGHEST
    )
    terms = terms.reshape(group_count, own_rows, terms.shape[1])
    added = sum_at_owner(terms, "front", 0)[0]
    return parent_part + added


def solution(mesh):
    placed = (
        P("front", None),
        P("front"),
        P("front", "grid", None),
        P(("front", "grid"), None),
        P(("front", "grid"), None),
    )
    return jax.shard_map(
        shards, mesh=mesh, in_specs=placed, out_specs=P(("front", "grid"), None), check_vma=False
    )
```

profile of v0, /device:TPU:1, one launch (start us, length us, event | category | flops | bytes accessed | tf_op | source)
XLA Modules:
  0.0 560.7 jit_solution(7659049847696991834)
XLA Ops:
  6.5 0.0 all-gather.3.cloned.1.call-start
  6.5 0.7 all-gather.3.cloned.1.call-update
  7.3 0.0 all-gather.5.cloned.1.call-start
  8.0 0.8 compare_and_fusion
  8.7 0.8 compare_select_fusion
  9.6 329.9 %all-gather.3.cloned.1.call-done = f32[16384,256]{1,0:T(8,128)} async-done(((f32[128,256]{1,0:T(8,128)}), f32[16384,256]{1,0:T(8,128)}) %all-gather.3.cloned.1.call-update) | async-done | bytes 16777232 | tf_op jit(solution)/shard_map/all_gather | solution.py:20
  339.5 37.3 %gather_fusion = f32[8192,256]{1,0:T(8,128)} fusion(f32[16384,256]{1,0:T(8,128)} %all-gather.3.cloned.1.call-done, s32[8192]{0:T(1024)S(1)} %broadcast_clamp_fusion), kind=kCustom, calls=%fused_computation | custom fusion | bytes 16809984 | tf_op jit(solution)/shard_map/jit(_take)/gather | solution.py:28
  376.8 0.0 copy-start
  376.8 21.5 %fusion.14 = f32[256,256]{0,1:T(8,128)} fusion(f32[1,256,8192]{2,1,0:T(8,128)} %param.7, f32[8192,256]{1,0:T(8,128)} %gather_fusion, pred[8192]{0:T(1024)(128)(4,1)S(1)} %compare_and_fusion, pred[256]{0:T(512)(128)(4,1)S(1)} %add_compare_fusion), kind=kOutput, calls=%fused_computation.11 | convolution fusion | flops 6444613632 | bytes 17047808 | tf_op jit(solution)/shard_map/dot_general | solution.py:29
  398.3 0.0 all-gather.5.cloned.1.call-update
  398.3 0.1 add_bitcast_fusion
  398.4 119.7 %all-gather.5.cloned.1.call-done = f32[8192,256]{0,1:T(8,128)} async-done(((f32[256,256]{0,1:T(8,128)}), f32[8192,256]{0,1:T(8,128)}) %all-gather.5.cloned.1.call-update) | async-done | bytes 8388624 | tf_op jit(solution)/shard_map/all_gather | solution.py:41
  518.1 0.0 copy-done
  518.1 10.6 %fusion = f32[512,256]{1,0:T(8,128)S(1)} fusion(f32[8192,256]{0,1:T(8,128)} %all-gather.5.cloned.1.call-done, s32[8192]{0:T(1024)S(1)} %bitcast.25, s32[512]{0:T(512)S(1)} %add_bitcast_fusion), kind=kOutput, calls=%fused_computation.1 | convolution fusion | flops 12889096192 | bytes 8947712 | tf_op jit(solution)/shard_map/dot_general | solution.py:48
  528.7 11.7 %all_to_all.5 = f32[4,1,128,256]{3,2,1,0:T(8,128)S(1)} all-to-all(f32[4,1,128,256]{3,2,1,0:T(8,128)S(1)} %bitcast.23), channel_id=1, replica_groups=mesh['front'=4,'grid'=32] {'front'}, dimensions={0} | all-to-all | bytes 1048576 | tf_op jit(solution)/shard_map/all_to_all | solution.py:15
  540.4 13.4 %convolution_add_fusion = f32[128,256]{1,0:T(8,128)} fusion(f32[128,256]{1,0:T(8,128)S(1)} %reduce_sum.9, f32[128,16384]{1,0:T(8,128)} %param.8, f32[16384,256]{1,0:T(8,128)} %all-gather.3.cloned.1.call-done), kind=kOutput, calls=%fused_computation.12 | convolution fusion | flops 6442483712 | bytes 25427968 | tf_op jit(solution)/shard_map/dot_general | solution.py:21
  (4 shorter events, 0.1 us)
Async XLA Ops:
  6.5 333.0 %all-gather.3.cloned.1.call-start = ((), (), s32[]{:S(2)}) async-start(), calls=%async_computation.1 | async-start | bytes 16908288 | tf_op jit(solution)/shard_map/all_gather | solution.py:20
  7.3 510.8 %all-gather.5.cloned.1.call-start = ((), (), s32[]{:S(2)}) async-start(), calls=%async_computation.2 | async-start | bytes 8650752 | tf_op jit(solution)/shard_map/all_gather | solution.py:41
  376.8 141.3 %copy-start = (s32[1,8192]{1,0:T(1,128)S(1)}, s32[1,8192]{1,0:T(1,128)}, u32[]{:S(2)}) copy-start(s32[1,8192]{1,0:T(1,128)} %param.5) | copy-start | bytes 98308
Sparse Core Ops, SparseCore 0:
  9.0 330.3 all-gather.2
  398.4 119.6 all-gather.4
where the time goes:
time: 561 us
  waiting for transfers between devices  450 us (80%)
  matrix products  45.5 us (8%)
  local copies, waits for them, and re-layouts  37.3 us (7%)
  between operations  14.1 us (3%)
  blocking collectives  11.7 us (2%)
    all_gather x1, waiting for transfers between devices, shards(): lax.all_gather(random, ('front', 'grid'), axis=0, tiled=True)  330 us
    all_gather x1, waiting for transfers between devices, shards(): group_sample = lax.all_gather(child_sample, 'grid', axis=0, tiled=True)  120 us
    gather x1, local copies, waits for them, and re-layouts, shards(): child_random = jnp.take(gathered_random, index_rows, axis=0)  37.3 us
    dot_general x1, matrix products, shards(): jnp.dot(update_front[0], child_random, preferred_element_type=jnp.float32...  21.5 us
    dot_general x1, matrix products, shards(): jnp.dot(front_matrix, gathered_random, preferred_element_type=jnp.float32...  13.4 us
    all_to_all x1, blocking collectives, sum_at_owner(): lax.all_to_all(split_up(array, dim, length), axis, 0, 0, tiled=True)  11.7 us
  transfers between devices with their start and end apart: 2, of which 2 were waited for; matrix products, arithmetic and copies ran while one was open for 0% of the time, Pallas kernels for 0%

commit v1 on v0

v1 whole, which is shorter than its diff:
```python
import functools

import jax
import jax.numpy as jnp
import numpy as np
from jax import lax
from jax.experimental import pallas as pl
from jax.experimental.pallas import tpu as pltpu
from jax.sharding import PartitionSpec as P

AXES = ("front", "grid")
SIDE = 4


def places():
    return [
        (x, y, z_hi * 2 + z_lo, core)
        for z_lo in range(2)
        for core in range(2)
        for z_hi in range(2)
        for y in range(SIDE)
        for x in range(SIDE)
    ]


PLACES = places()
DEVICE = {place: i for i, place in enumerate(PLACES)}
BITS = [(z, y, x) for z in range(2) for y in range(2) for x in range(2)]


def cube_of(v, shift):
    return ((v - shift) % SIDE) // 2


def near_groups():
    groups = []
    for core in range(2):
        for cube in BITS:
            groups.append(
                [
                    DEVICE[tuple((2 * c + b + core) % SIDE for c, b in zip(cube[::-1], bit[::-1])) + (core,)]
                    for bit in BITS
                ]
            )
    return groups


def far_groups():
    groups = []
    for core in range(2):
        for cube in BITS:
            members = [DEVICE[tuple((2 * c + b + 1 - core) % SIDE for c, b in zip(cube[::-1], bit[::-1])) + (core,)] for bit in BITS]
            members.sort(key=lambda d: tuple(cube_of(PLACES[d][i], core) for i in (2, 1, 0)))
            groups.append(members)
    return groups


NEAR = near_groups()
FAR = far_groups()
CORES = [(i, DEVICE[(x, y, z, 1 - core)]) for i, (x, y, z, core) in enumerate(PLACES)]
LAYERS = [(i, DEVICE[(x, y, z ^ 1, core)]) for i, (x, y, z, core) in enumerate(PLACES)]


def map_rows():
    rows = np.zeros((len(PLACES), 16), np.int32)
    for group in NEAR:
        for d in group:
            for j, m in enumerate(group):
                x, y, z, _ = PLACES[m]
                for other in range(2):
                    layer = (z ^ PLACES[d][2]) & 1
                    rows[d, 2 * j + other] = (layer * 2 + other) * 32 + (z // 2) * 16 + y * 4 + x
    return rows


MAP_ROWS = map_rows()


def swap_cores(a):
    return lax.ppermute(a, AXES, CORES)


def spread(a, groups):
    copies = jnp.broadcast_to(a[None], (len(groups[0]), *a.shape))
    return lax.all_to_all(copies, AXES, 0, 0, tiled=True, axis_index_groups=groups)


def split2(a):
    high = a.astype(jnp.bfloat16)
    return high, (a - high.astype(jnp.float32)).astype(jnp.bfloat16)


def dot3(a, b):
    n = b.shape[1]
    a_high, a_low = split2(a)
    b_high, b_low = split2(b)
    both = jnp.dot(a_high, jnp.concatenate([b_high, b_low], axis=1), preferred_element_type=jnp.float32)
    return both[:, :n] + both[:, n:] + jnp.dot(a_low, b_high, preferred_element_type=jnp.float32)


def child_kernel(depth, own_at, other_at, random_ref, own_ref, other_ref, own_out, other_out, held, own_rows, other_rows, sem):
    step = pl.program_id(0)
    last = pl.num_programs(0) - 1
    place = lax.broadcasted_iota(jnp.int32, (8, 128), 0)

    def gather(at, chunk, rows):
        base = chunk * depth
        for j in range(0, depth, 8):
            tile = jnp.broadcast_to(held[pl.ds(at[base + j], 1), :], (8, 128))
            for t in range(1, 8):
                row = jnp.broadcast_to(held[pl.ds(at[base + j + t], 1), :], (8, 128))
                tile = jnp.where(place == t, row, tile)
            rows[j : j + 8, :] = tile

    @pl.when(step == 0)
    def _():
        copy = pltpu.make_async_copy(random_ref, held, sem)
        copy.start()
        copy.wait()
        own_out[...] = jnp.zeros_like(own_out)
        other_out[...] = jnp.zeros_like(other_out)
        gather(own_at, 0, own_rows.at[0])
        gather(other_at, 0, other_rows.at[0])

    slot = lax.rem(step, 2)
    later = jnp.minimum(step + 1, last)
    gather(own_at, later, own_rows.at[1 - slot])
    gather(other_at, later, other_rows.at[1 - slot])
    own_out[...] += dot3(own_ref[...], own_rows[slot])
    other_out[...] += dot3(other_ref[...], other_rows[slot])


def child_products(own_at, other_at, random, own, other, depth=1024):
    rows, inner = own.shape
    width = random.shape[1]
    out = jax.ShapeDtypeStruct((rows, width), jnp.float32)
    block = pl.BlockSpec((rows, depth), lambda k, *_: (0, k))
    whole = pl.BlockSpec((rows, width), lambda k, *_: (0, 0))
    return pl.pallas_call(
        functools.partial(child_kernel, depth),
        out_shape=(out, out),
        grid_spec=pltpu.PrefetchScalarGridSpec(
            num_scalar_prefetch=2,
            grid=(inner // depth,),
            in_specs=[pl.BlockSpec(memory_space=pl.ANY), block, block],
            out_specs=[whole, whole],
            scratch_shapes=[
                pltpu.VMEM(random.shape, jnp.float32),
                pltpu.VMEM((2, depth, width), jnp.float32),
                pltpu.VMEM((2, depth, width), jnp.float32),
                pltpu.SemaphoreType.DMA,
            ],
        ),
        compiler_params=pltpu.CompilerParams(vmem_limit_bytes=30 << 20),
        cost_estimate=pl.CostEstimate(flops=12 * rows * inner * width, bytes_accessed=24 << 20, transcendentals=0),
        name="child",
    )(own_at, other_at, random, own, other)


def front_kernel(depth, blocks, random_ref, own_ref, other_ref, out, held, sem):
    step = pl.program_id(0)

    @pl.when(step == 0)
    def _():
        copy = pltpu.make_async_copy(random_ref, held, sem)
        copy.start()
        copy.wait()
        out[...] = jnp.zeros_like(out)

    count = depth // 128
    rows = [held[pl.ds(pl.multiple_of(blocks[step * count + i] * 128, 128), 128), :] for i in range(count)]
    out[...] += dot3(jnp.concatenate([own_ref[...], other_ref[...]], axis=0), jnp.concatenate(rows, axis=0))


def front_products(blocks, random, own, other, depth=1024):
    rows, inner = own.shape
    width = random.shape[1]
    block = pl.BlockSpec((rows, depth), lambda k, *_: (0, k))
    return pl.pallas_call(
        functools.partial(front_kernel, depth),
        out_shape=jax.ShapeDtypeStruct((2 * rows, width), jnp.float32),
        grid_spec=pltpu.PrefetchScalarGridSpec(
            num_scalar_prefetch=1,
            grid=(inner // depth,),
            in_specs=[pl.BlockSpec(memory_space=pl.ANY), block, block],
            out_specs=pl.BlockSpec((2 * rows, width), lambda k, *_: (0, 0)),
            scratch_shapes=[pltpu.VMEM(random.shape, jnp.float32), pltpu.SemaphoreType.DMA],
        ),
        compiler_params=pltpu.CompilerParams(vmem_limit_bytes=30 << 20),
        cost_estimate=pl.CostEstimate(flops=12 * rows * inner * width, bytes_accessed=24 << 20, transcendentals=0),
        name="front",
    )(blocks, random, own, other)


def coordinates(block):
    front, grid = block >> 5, block & 31
    return grid & 3, (grid >> 2) & 3, (grid >> 4) * 2 + (front >> 1), front & 1


def held_block(block, core):
    x, y, z, owner = coordinates(block)
    x, y, z = (x - core) & 3, (y - core) & 3, (z - core) & 3
    far = (z >> 1) * 4 + (y >> 1) * 2 + (x >> 1)
    near = (z & 1) * 4 + (y & 1) * 2 + (x & 1)
    return (far * 8 + near) * 2 + (owner ^ core)


def shards(index_map, lengths, update_front, front_matrix, random):
    me = lax.axis_index("front") * 32 + lax.axis_index("grid")
    core = lax.axis_index("front") & 1
    width = random.shape[1] // 2
    own_rows = random.shape[0]
    sample_rows = update_front.shape[1]

    own_update, own_front = update_front[0], front_matrix
    left, right = random[:, :width], random[:, width:]
    kept = jnp.where(core == 0, left, right)
    given = jnp.where(core == 0, right, left)
    near = spread(jnp.concatenate([kept, swap_cores(given)], axis=0), NEAR)
    other_update = swap_cores(own_update)
    other_front = swap_cores(own_front)
    own_map = jnp.concatenate([index_map[0], jnp.broadcast_to(lengths, (128,))])
    maps = jnp.stack([own_map, swap_cores(own_map)])
    gathered = spread(near.reshape(-1, width), FAR).reshape(-1, width)

    live = maps[:, -1]
    maps = maps[:, :-128]
    at = held_block(maps >> 7, core) * 128 + (maps & 127)
    own_sample, other_sample = child_products(at[0], at[1], gathered, own_update, other_update)
    first = lax.axis_index("grid") * sample_rows
    rows = first + jnp.arange(sample_rows, dtype=jnp.int32)
    samples = jnp.where((rows[None, :] < live[:, None])[:, :, None], jnp.stack([own_sample, other_sample]), jnp.float32(0.0))
    cube = spread(samples, NEAR).reshape(-1, width)

    blocks = held_block(jnp.arange(WHOLE_BLOCKS, dtype=jnp.int32), core)
    front = front_products(blocks, gathered, own_front, other_front)

    layers = jnp.concatenate([maps, lax.ppermute(maps, AXES, LAYERS)]).reshape(-1, sample_rows)
    wanted = lax.dynamic_index_in_dim(jnp.asarray(MAP_ROWS), me, 0, keepdims=False)
    targets = jnp.take(layers, wanted, axis=0).reshape(-1)
    x, y, z, owner = coordinates(targets >> 7)
    grid = lax.axis_index("grid")
    mine = (grid & 3, (grid >> 2) & 3, (grid >> 4) * 2 + (lax.axis_index("front") >> 1))
    ours = functools.reduce(
        jnp.logical_and,
        [(((v - 1 + core) & 3) >> 1) == (((m - 1 + core) & 3) >> 1) for v, m in zip((x, y, z), mine)],
    )
    member = sum(((((v - core) & 3) >> 1) << i) for i, v in enumerate((x, y, z)))
    slots = jnp.where(ours, (member * 2 + (owner ^ core)) * own_rows + (targets & (own_rows - 1)), -1)
    chosen = (jnp.arange(16 * own_rows, dtype=jnp.int32)[:, None] == slots[None, :]).astype(jnp.bfloat16)
    rounded = lax.reduce_precision(cube, 8, 7)
    high, low = rounded.astype(jnp.bfloat16), (cube - rounded).astype(jnp.bfloat16)
    terms = jnp.dot(chosen, jnp.concatenate([high, low], axis=1), preferred_element_type=jnp.float32)
    terms = (terms[:, :width] + terms[:, width:]).reshape(8, 2 * own_rows, width)
    parts = lax.all_to_all(terms, AXES, 0, 0, tiled=True, axis_index_groups=FAR)
    total = front + jnp.sum(parts, axis=0)
    mine_half, other_half = total[:own_rows], swap_cores(total[own_rows:])
    return jnp.where(
        core == 0,
        jnp.concatenate([mine_half, other_half], axis=1),
        jnp.concatenate([other_half, mine_half], axis=1),
    )


WHOLE_BLOCKS = len(PLACES)


def solution(mesh):
    placed = (
        P("front", None),
        P("front"),
        P("front", "grid", None),
        P(("front", "grid"), None),
        P(("front", "grid"), None),
    )
    return jax.shard_map(
        shards, mesh=mesh, in_specs=placed, out_specs=P(("front", "grid"), None), check_vma=False
    )
```

time: 561 us -> 177 us (0.32)
  waiting for transfers between devices: 450 us -> 67.4 us
  Pallas kernels: 0 us -> 40.9 us
  matrix products: 45.5 us -> 6.44 us
  local copies, waits for them, and re-layouts: 37.3 us -> 12.9 us
  starting transfers between devices: 0.04 us -> 24.2 us
  between operations: 14.1 us -> 0.84 us
  blocking collectives: 11.7 us -> 18 us
    all_gather x2 -> x0, waiting for transfers between devices: 450 us -> none  [the longest x1 330 us: shards(): lax.all_gather(random, ('front', 'grid'), axis=0, tiled=True)]
    all_to_all x0 -> x3, waiting for transfers between devices: none -> 58.9 us  [the longest x2 58.9 us: spread(): lax.all_to_all(copies, AXES, 0, 0, tiled=True, axis_index_groups=groups)]
    pallas_call x0 -> x2, Pallas kernels: none -> 40.9 us  [the longest x1 24 us: child_products(): pl.pallas_call(functools.partial(child_kernel, depth), out_shape=(out, ou...]
    dot_general x3 -> x1, matrix products: 45.5 us -> 6.44 us  [shards(): jnp.dot(chosen, jnp.concatenate([high, low], axis=1), preferred_element_t...]
    gather x1, local copies, waits for them, and re-layouts: 37.3 us -> 0.58 us  [shards(): targets = jnp.take(layers, wanted, axis=0).reshape(-1)]
    all_to_all x0 -> x3, starting transfers between devices: none -> 19.4 us  [the longest x2 14.9 us: spread(): lax.all_to_all(copies, AXES, 0, 0, tiled=True, axis_index_groups=groups)]
    ppermute x0 -> x6, waiting for transfers between devices: none -> 8.51 us  [the longest x1 6.13 us: shards(): lax.ppermute(maps, AXES, LAYERS)]
    unnamed x2 -> x7, local copies, waits for them, and re-layouts: 0.01 us -> 6.77 us
  transfers between devices with their start and end apart: 2 -> 9, of which waited for: 2 -> 6; matrix products, arithmetic and copies ran while one was open for 0% -> 9% of each run, Pallas kernels for 0% -> 23%
where the time goes in v1:
time: 177 us; the launch traced here: 176 us
  waiting for transfers between devices  67.4 us (38%)
  Pallas kernels  40.9 us (23%)
  starting transfers between devices  24.2 us (14%)
  blocking collectives  18 us (10%)
  local copies, waits for them, and re-layouts  12.9 us (7%)
  matrix products  6.44 us (4%)
  other arithmetic  5.4 us (3%)
    all_to_all x2, waiting for transfers between devices, spread(): lax.all_to_all(copies, AXES, 0, 0, tiled=True, axis_index_groups=groups)  58.9 us
    pallas_call x1, Pallas kernels, child_products(): pl.pallas_call(functools.partial(child_kernel, depth), out_shape=(out, ou...  24 us
    all_to_all x1, blocking collectives, spread(): lax.all_to_all(copies, AXES, 0, 0, tiled=True, axis_index_groups=groups)  18 us
    pallas_call x1, Pallas kernels, front_products(): pl.pallas_call(functools.partial(front_kernel, depth), out_shape=jax.Shap...  16.9 us
    all_to_all x2, starting transfers between devices, spread(): lax.all_to_all(copies, AXES, 0, 0, tiled=True, axis_index_groups=groups)  14.9 us
    unnamed x7, local copies, waits for them, and re-layouts  6.77 us
    dot_general x1, matrix products, shards(): jnp.dot(chosen, jnp.concatenate([high, low], axis=1), preferred_element_t...  6.44 us
    ppermute x1, waiting for transfers between devices, shards(): lax.ppermute(maps, AXES, LAYERS)  6.13 us
  transfers between devices with their start and end apart: 9, of which 6 were waited for; matrix products, arithmetic and copies ran while one was open for 9% of the time, Pallas kernels for 23%

profile of v1, /device:TPU:1, one launch (start us, length us, event | category | flops | bytes accessed | tf_op | source)
XLA Modules:
  0.0 176.1 jit_solution(17348279870122808349)
XLA Ops:
  0.0 0.9 slice_select_fusion.1
  0.9 1.5 collective-permute-start
  2.4 0.1 collective-permute-start.4
  2.5 0.8 collective-permute-done
  3.3 0.1 broadcast_in_dim.52
  3.4 18.0 %all_to_all.20 = f32[8,256,128]{2,1,0:T(8,128)S(1)} all-to-all(f32[8,256,128]{2,1,0:T(8,128)S(1)} %broadcast_in_dim.52), channel_id=1, replica_groups={{0,1,4,5,64,65,68,69},{2,3,6,7,66,67,70,71},{8,9,12,13,72,73,76,77},{10..., dimensions={0} | all-to-all | bytes 2097152 | tf_op jit(solution)/shard_map/all_to_all | solution.py:85
  21.3 3.8 %broadcast_in_dim.54 = f32[8,2048,128]{2,1,0:T(8,128)} broadcast(f32[2048,128]{1,0:T(8,128)S(1)} %bitcast.29), dimensions={1,2} | broadcast | bytes 9437184 | tf_op jit(solution)/shard_map/broadcast_in_dim | solution.py:84
  25.1 0.0 copy-start.2
  25.1 5.4 %all-to-all-start.1 = ((f32[8,2048,128]{2,1,0:T(8,128)}), f32[8,2048,128]{2,1,0:T(8,128)}, u32[]{:S(2)}, u32[]{:S(2)}) async-start(f32[8,2048,128]{2,1,0:T(8,128)} %broadcast_in_dim.54), calls=%async_computation.1 | async-start | bytes 16777216 | tf_op jit(solution)/shard_map/all_to_all | solution.py:85
  31.1 0.0 copy-done.2
  31.2 0.1 collective-permute-start.2
  31.3 0.5 collective-permute-start.1
  31.8 0.7 collective-permute-done.2
  32.5 0.2 fusion.9
  32.7 0.1 broadcast_compare_fusion
  32.7 0.4 and_add_fusion
  33.1 0.1 fusion.30
  33.2 54.3 %all-to-all-done.1 = f32[8,2048,128]{2,1,0:T(8,128)} async-done(((f32[8,2048,128]{2,1,0:T(8,128)}), f32[8,2048,128]{2,1,0:T(8,128)}, u32[]{:S(2)}, u32[]{:S(2)}) %all-to-all-start.1) | async-done | bytes 8388640 | tf_op jit(solution)/shard_map/all_to_all | solution.py:85
  87.5 0.0 collective-permute-done.4.other_ref
  87.5 0.0 copy-start
  87.5 3.4 %copy-done = f32[1,256,8192]{2,1,0:T(8,128)S(1)} copy-done((f32[1,256,8192]{2,1,0:T(8,128)S(1)}, f32[1,256,8192]{2,1,0:T(8,128)}, u32[]{:S(2)}) %copy-start) | copy-done | bytes 8388632
  90.9 24.0 %child.1 = (f32[256,128]{1,0:T(8,128)S(1)}, f32[256,128]{1,0:T(8,128)S(1)}) custom-call(s32[8192]{0:T(1024)S(1)} %bitcast.26, s32[8192]{0:T(1024)S(1)} %bitcast.25, f32[16384,128]{1,0:T(8,128)} %bitcast.1.random_ref, f32[256,8192]{1,0:T(8,128)S(1)} %bitcast.24, f32[256,8192]{1,0:T(8,128)} %collective-permute-done.4.other_ref), custom_call_target="tpu_custom_call" | custom-call | flops 3221225472 | bytes 25165824 | tf_op jit(solution)/shard_map/child/pallas_call | solution.py:139
  114.9 0.1 maximum_select_fusion
  115.1 1.5 broadcast_in_dim.60
  116.6 9.5 %all-to-all-start.2 = ((f32[8,2,256,128]{3,2,1,0:T(8,128)}), f32[8,2,256,128]{3,2,1,0:T(8,128)S(1)}, u32[]{:S(2)}, u32[]{:S(2)}) async-start(f32[8,2,256,128]{3,2,1,0:T(8,128)} %broadcast_in_dim.60), calls=%async_computation.2 | async-start | bytes 4194304 | tf_op jit(solution)/shard_map/all_to_all | solution.py:85
  126.1 0.7 fusion.26
  126.8 0.3 collective-permute-start.3
  127.0 0.7 compare_and_fusion
  127.7 6.1 %collective-permute-done.3 = s32[2,8192]{1,0:T(2,128)S(1)} collective-permute-done((s32[2,8192]{1,0:T(2,128)S(1)}, s32[2,8192]{1,0:T(2,128)S(1)}, u32[]{:S(2)}, u32[]{:S(2)}) %collective-permute-start.3) | collective-permute-done | bytes 65568 | tf_op jit(solution)/shard_map/ppermute | solution.py:238
  133.9 0.1 pad_add_fusion
  133.9 0.1 reshape.180
  134.0 0.6 gather_fusion
  134.6 0.1 select_bitcast_fusion
  134.7 4.6 %all-to-all-done.2 = f32[8,2,256,128]{3,2,1,0:T(8,128)S(1)} async-done(((f32[8,2,256,128]{3,2,1,0:T(8,128)}), f32[8,2,256,128]{3,2,1,0:T(8,128)S(1)}, u32[]{:S(2)}, u32[]{:S(2)}) %all-to-all-start.2) | async-done | bytes 2097184 | tf_op jit(solution)/shard_map/all_to_all | solution.py:85
  139.3 0.3 reduce-precision_convert_fusion
  139.7 6.4 %fusion = f32[2048,256]{1,0:T(8,128)S(1)} fusion(s32[4096]{0:T(1024)S(1)} %bitcast.31, bf16[4096,128]{1,0:T(8,128)(2,1)S(1)} %get-tuple-element.12, bf16[4096,128]{1,0:T(8,128)(2,1)S(1)} %get-tuple-element.11), kind=kOutput, calls=%fused_computation.2 | convolution fusion | flops 4307550208 | bytes 4210688 | tf_op jit(solution)/shard_map/dot_general | solution.py:253
  146.1 1.1 slice_add_fusion
  147.2 4.5 %all-to-all-start.3 = ((f32[8,256,128]{2,1,0:T(8,128)}), f32[8,256,128]{2,1,0:T(8,128)S(1)}, u32[]{:S(2)}, u32[]{:S(2)}) async-start(f32[8,256,128]{2,1,0:T(8,128)} %bitcast.13), calls=%async_computation.3 | async-start | bytes 2097152 | tf_op jit(solution)/shard_map/all_to_all | solution.py:255
  151.8 0.0 collective-permute-done.1.other_ref
  151.8 0.0 copy-start.1
  151.8 3.4 %copy-done.1 = f32[128,16384]{1,0:T(8,128)S(1)} copy-done((f32[128,16384]{1,0:T(8,128)S(1)}, f32[128,16384]{1,0:T(8,128)}, u32[]{:S(2)}) %copy-start.1) | copy-done | bytes 8388632
  155.1 16.9 %front.1 = f32[256,128]{1,0:T(8,128)S(1)} custom-call(s32[128]{0:T(128)S(1)} %fusion.17.blocks, f32[16384,128]{1,0:T(8,128)} %bitcast.1.random_ref, f32[128,16384]{1,0:T(8,128)S(1)} %copy-done.1, f32[128,16384]{1,0:T(8,128)} %collective-permute-done.1.other_ref), custom_call_target="tpu_custom_call" | custom-call | flops 3221225472 | bytes 25165824 | tf_op jit(solution)/shard_map/front/pallas_call | solution.py:179
  172.1 0.0 all-to-all-done.3
  172.1 0.1 reduce_sum.9
  172.2 2.3 %collective-permute-start.5 = (f32[128,128]{1,0:T(8,128)S(1)}, f32[128,128]{1,0:T(8,128)S(1)}, u32[]{:S(2)}, u32[]{:S(2)}) collective-permute-start(f32[128,128]{1,0:T(8,128)S(1)} %get-tuple-element.14), channel_id=1, source_target_pairs={{0,32},{1,33},{2,34},{3,35},{4,36},{5,37},{6,38},{7,39},{8,40},{9,... | collective-permute-start | bytes 196616 | tf_op jit(solution)/shard_map/ppermute | solution.py:80
  174.5 0.9 collective-permute-done.5
  175.4 0.7 maximum_select_fusion.1
  (10 shorter events, 0.1 us)
Async XLA Ops:
  0.9 2.4 %collective-permute-start = (f32[128,128]{1,0:T(8,128)S(1)}, f32[128,128]{1,0:T(8,128)S(1)}, u32[]{:S(2)}, u32[]{:S(2)}) collective-permute-start(f32[128,128]{1,0:T(8,128)S(1)} %get-tuple-element.16), channel_id=1, source_target_pairs={{0,32},{1,33},{2,34},{3,35},{4,36},{5,37},{6,38},{7,39},{8,40},{9,... | collective-permute-start | bytes 196616 | tf_op jit(solution)/shard_map/ppermute | solution.py:80
  2.4 85.1 %collective-permute-start.4 = (f32[256,8192]{1,0:T(8,128)}, f32[256,8192]{1,0:T(8,128)}, u32[]{:S(2)}, u32[]{:S(2)}) collective-permute-start(f32[256,8192]{1,0:T(8,128)} %bitcast.23), channel_id=1, source_target_pairs={{0,32},{1,33},{2,34},{3,35},{4,36},{5,37},{6,38},{7,39},{8,40},{9,... | collective-permute-start | bytes 25165832 | tf_op jit(solution)/shard_map/ppermute | solution.py:80
  25.1 6.0 %copy-start.2 = (s32[1,8192]{1,0:T(1,128)S(1)}, s32[1,8192]{1,0:T(1,128)}, u32[]{:S(2)}) copy-start(s32[1,8192]{1,0:T(1,128)} %param.6) | copy-start | bytes 98308
  25.1 62.4 %all-to-all-start.1 = ((f32[8,2048,128]{2,1,0:T(8,128)}), f32[8,2048,128]{2,1,0:T(8,128)}, u32[]{:S(2)}, u32[]{:S(2)}) async-start(f32[8,2048,128]{2,1,0:T(8,128)} %broadcast_in_dim.54), calls=%async_computation.1 | async-start | bytes 16777216 | tf_op jit(solution)/shard_map/all_to_all | solution.py:85
  31.2 1.3 collective-permute-start.2
  31.3 120.5 %collective-permute-start.1 = (f32[128,16384]{1,0:T(8,128)}, f32[128,16384]{1,0:T(8,128)}, u32[]{:S(2)}, u32[]{:S(2)}) collective-permute-start(f32[128,16384]{1,0:T(8,128)} %own_ref.1), channel_id=1, source_target_pairs={{0,32},{1,33},{2,34},{3,35},{4,36},{5,37},{6,38},{7,39},{8,40},{9,... | collective-permute-start | bytes 25165832 | tf_op jit(solution)/shard_map/ppermute | solution.py:80
  87.5 3.4 %copy-start = (f32[1,256,8192]{2,1,0:T(8,128)S(1)}, f32[1,256,8192]{2,1,0:T(8,128)}, u32[]{:S(2)}) copy-start(f32[1,256,8192]{2,1,0:T(8,128)} %param.8) | copy-start | bytes 25165828
  116.6 22.7 %all-to-all-start.2 = ((f32[8,2,256,128]{3,2,1,0:T(8,128)}), f32[8,2,256,128]{3,2,1,0:T(8,128)S(1)}, u32[]{:S(2)}, u32[]{:S(2)}) async-start(f32[8,2,256,128]{3,2,1,0:T(8,128)} %broadcast_in_dim.60), calls=%async_computation.2 | async-start | bytes 4194304 | tf_op jit(solution)/shard_map/all_to_all | solution.py:85
  126.8 7.1 %collective-permute-start.3 = (s32[2,8192]{1,0:T(2,128)S(1)}, s32[2,8192]{1,0:T(2,128)S(1)}, u32[]{:S(2)}, u32[]{:S(2)}) collective-permute-start(s32[2,8192]{1,0:T(2,128)S(1)} %get-tuple-element.10), channel_id=1, source_target_pairs={{0,64},{1,65},{2,66},{3,67},{4,68},{5,69},{6,70},{7,71},{8,72},{9,... | collective-permute-start | bytes 196616 | tf_op jit(solution)/shard_map/ppermute | solution.py:238
  147.2 24.9 %all-to-all-start.3 = ((f32[8,256,128]{2,1,0:T(8,128)}), f32[8,256,128]{2,1,0:T(8,128)S(1)}, u32[]{:S(2)}, u32[]{:S(2)}) async-start(f32[8,256,128]{2,1,0:T(8,128)} %bitcast.13), calls=%async_computation.3 | async-start | bytes 2097152 | tf_op jit(solution)/shard_map/all_to_all | solution.py:255
  151.8 3.4 %copy-start.1 = (f32[128,16384]{1,0:T(8,128)S(1)}, f32[128,16384]{1,0:T(8,128)}, u32[]{:S(2)}) copy-start(f32[128,16384]{1,0:T(8,128)} %own_ref.1) | copy-start | bytes 25165828
  172.2 3.2 %collective-permute-start.5 = (f32[128,128]{1,0:T(8,128)S(1)}, f32[128,128]{1,0:T(8,128)S(1)}, u32[]{:S(2)}, u32[]{:S(2)}) collective-permute-start(f32[128,128]{1,0:T(8,128)S(1)} %get-tuple-element.14), channel_id=1, source_target_pairs={{0,32},{1,33},{2,34},{3,35},{4,36},{5,37},{6,38},{7,39},{8,40},{9,... | collective-permute-start | bytes 196616 | tf_op jit(solution)/shard_map/ppermute | solution.py:80

commit v2 on v1

v2 whole, which is shorter than its diff:
```python
import functools

import jax
import jax.numpy as jnp
import numpy as np
from jax import lax
from jax.experimental import pallas as pl
from jax.experimental.pallas import tpu as pltpu
from jax.sharding import PartitionSpec as P

AXES = ("front", "grid")
SIDE = 4


def places():
    return [
        (x, y, z_hi * 2 + z_lo, core)
        for z_lo in range(2)
        for core in range(2)
        for z_hi in range(2)
        for y in range(SIDE)
        for x in range(SIDE)
    ]


PLACES = places()
DEVICE = {place: i for i, place in enumerate(PLACES)}
BITS = [(z, y, x) for z in range(2) for y in range(2) for x in range(2)]


def cube_of(v, shift):
    return ((v - shift) % SIDE) // 2


def near_groups():
    groups = []
    for core in range(2):
        for cube in BITS:
            groups.append(
                [
                    DEVICE[tuple((2 * c + b + core) % SIDE for c, b in zip(cube[::-1], bit[::-1])) + (core,)]
                    for bit in BITS
                ]
            )
    return groups


def far_groups():
    groups = []
    for core in range(2):
        for cube in BITS:
            members = [DEVICE[tuple((2 * c + b + 1 - core) % SIDE for c, b in zip(cube[::-1], bit[::-1])) + (core,)] for bit in BITS]
            members.sort(key=lambda d: tuple(cube_of(PLACES[d][i], core) for i in (2, 1, 0)))
            groups.append(members)
    return groups


NEAR = near_groups()
FAR = far_groups()
CORES = [(i, DEVICE[(x, y, z, 1 - core)]) for i, (x, y, z, core) in enumerate(PLACES)]
LAYERS = [(i, DEVICE[(x, y, z ^ 1, core)]) for i, (x, y, z, core) in enumerate(PLACES)]


def map_rows():
    rows = np.zeros((len(PLACES), 16), np.int32)
    for group in NEAR:
        for d in group:
            for j, m in enumerate(group):
                x, y, z, _ = PLACES[m]
                for other in range(2):
                    layer = (z ^ PLACES[d][2]) & 1
                    rows[d, 2 * j + other] = (layer * 2 + other) * 32 + (z // 2) * 16 + y * 4 + x
    return rows


MAP_ROWS = map_rows()


def swap_cores(a):
    return lax.ppermute(a, AXES, CORES)


def spread(a, groups):
    copies = jnp.broadcast_to(a[None], (len(groups[0]), *a.shape))
    return lax.all_to_all(copies, AXES, 0, 0, tiled=True, axis_index_groups=groups)


def halves(a):
    high = lax.reduce_precision(a, 8, 7)
    return high.astype(jnp.bfloat16), (a - high).astype(jnp.bfloat16)


def held_halves(rows):
    high = rows.astype(jnp.bfloat16)
    low = (rows - high.astype(jnp.float32)).astype(jnp.bfloat16)
    return high, low


def joined(p):
    m, n = p.shape[0] // 2, p.shape[1] // 2
    return (p[:m, :n] + p[m:, :n]) + (p[:m, n:] + p[m:, n:])


def child_kernel(depth, at, random, update, out, even, odd, fetched, sems):
    chunks = update.shape[1] // depth
    place = lax.broadcasted_iota(jnp.int32, (8, 128), 0)

    def fetch(chunk, slot):
        columns = pl.ds(pl.multiple_of(chunk * depth, depth), depth)
        return pltpu.make_async_copy(update.at[:, columns], fetched.at[slot], sems.at[slot])

    def gather(chunk, rows):
        base = chunk * depth
        for j in range(0, depth, 8):
            tile = jnp.broadcast_to(random[pl.ds(at[base + j], 1), :], (8, 128))
            for t in range(1, 8):
                row = jnp.broadcast_to(random[pl.ds(at[base + j + t], 1), :], (8, 128))
                tile = jnp.where(place == t, row, tile)
            rows[j : j + 8, :] = tile

    def product(slot, rows):
        stacked = jnp.concatenate(held_halves(fetched[slot]), axis=0)
        columns = jnp.concatenate(held_halves(rows[...]), axis=1)
        out[...] += joined(jnp.dot(stacked, columns, preferred_element_type=jnp.float32))

    fetch(0, 0).start()
    fetch(1, 1).start()
    gather(0, even)
    out[...] = jnp.zeros_like(out)

    def pair(i, carry):
        fetch(2 * i, 0).wait()
        gather(2 * i + 1, odd)
        product(0, even)

        @pl.when(2 * i + 2 < chunks)
        def _():
            fetch(2 * i + 2, 0).start()

        fetch(2 * i + 1, 1).wait()
        gather(jnp.minimum(2 * i + 2, chunks - 1), even)
        product(1, odd)

        @pl.when(2 * i + 3 < chunks)
        def _():
            fetch(2 * i + 3, 1).start()

        return carry

    lax.fori_loop(0, chunks // 2, pair, 0)


def child_product(at, random, update, limit, depth=1024):
    rows, inner = update.shape
    width = random.shape[1]
    whole = pl.BlockSpec(memory_space=pltpu.VMEM)
    return pl.pallas_call(
        functools.partial(child_kernel, depth),
        out_shape=jax.ShapeDtypeStruct((rows, width), jnp.float32),
        in_specs=[pl.BlockSpec(memory_space=pltpu.SMEM), whole, pl.BlockSpec(memory_space=pl.ANY)],
        out_specs=whole,
        scratch_shapes=[
            pltpu.VMEM((depth, width), jnp.float32),
            pltpu.VMEM((depth, width), jnp.float32),
            pltpu.VMEM((2, rows, depth), jnp.float32),
            pltpu.SemaphoreType.DMA((2,)),
        ],
        compiler_params=pltpu.CompilerParams(vmem_limit_bytes=limit),
        cost_estimate=pl.CostEstimate(flops=8 * rows * inner * width, bytes_accessed=16 << 20, transcendentals=0),
        name="child",
    )(at, random, update)


def front_kernel(depth, blocks, random, own, other, out):
    step = pl.program_id(0)
    count = depth // 128

    @pl.when(step == 0)
    def _():
        out[...] = jnp.zeros_like(out)

    rows = [random[pl.ds(pl.multiple_of(blocks[step * count + i] * 128, 128), 128), :] for i in range(count)]
    columns = jnp.concatenate(held_halves(jnp.concatenate(rows, axis=0)), axis=1)
    stacked = jnp.concatenate(held_halves(jnp.concatenate([own[...], other[...]], axis=0)), axis=0)
    out[...] += joined(jnp.dot(stacked, columns, preferred_element_type=jnp.float32))


def front_product(blocks, random, own, other, depth=2048):
    rows, inner = own.shape
    width = random.shape[1]
    block = pl.BlockSpec((rows, depth), lambda k, *_: (0, k))
    return pl.pallas_call(
        functools.partial(front_kernel, depth),
        out_shape=jax.ShapeDtypeStruct((2 * rows, width), jnp.float32),
        grid_spec=pltpu.PrefetchScalarGridSpec(
            num_scalar_prefetch=1,
            grid=(inner // depth,),
            in_specs=[pl.BlockSpec(random.shape, lambda k, *_: (0, 0), pipeline_mode=pl.Buffered(1)), block, block],
            out_specs=pl.BlockSpec((2 * rows, width), lambda k, *_: (0, 0)),
        ),
        compiler_params=pltpu.CompilerParams(vmem_limit_bytes=VMEM_LIMIT),
        cost_estimate=pl.CostEstimate(flops=16 * rows * inner * width, bytes_accessed=24 << 20, transcendentals=0),
        name="front",
    )(blocks, random, own, other)


def coordinates(block):
    front, grid = block >> 5, block & 31
    return grid & 3, (grid >> 2) & 3, (grid >> 4) * 2 + (front >> 1), front & 1


def held_block(block, core):
    x, y, z, owner = coordinates(block)
    x, y, z = (x - core) & 3, (y - core) & 3, (z - core) & 3
    far = (z >> 1) * 4 + (y >> 1) * 2 + (x >> 1)
    near = (z & 1) * 4 + (y & 1) * 2 + (x & 1)
    return (far * 8 + near) * 2 + (owner ^ core)


def shards(index_map, lengths, update_front, front_matrix, random):
    me = lax.axis_index("front") * 32 + lax.axis_index("grid")
    core = lax.axis_index("front") & 1
    width = random.shape[1] // 2
    own_rows = random.shape[0]
    sample_rows = update_front.shape[1]

    own_update, own_front = update_front[0], front_matrix
    left, right = random[:, :width], random[:, width:]
    kept = jnp.where(core == 0, left, right)
    given = jnp.where(core == 0, right, left)
    near = spread(jnp.concatenate([kept, swap_cores(given)], axis=0), NEAR)
    other_update = swap_cores(own_update)

    own_map = jnp.concatenate([index_map[0], jnp.broadcast_to(lengths, (128,))])
    maps = jnp.stack([own_map, swap_cores(own_map)])
    live = maps[:, -1]
    maps = maps[:, :-128]
    at = held_block(maps >> 7, core) * 128 + (maps & 127)
    own_at, other_at = at[0], at[1]
    first = lax.axis_index("grid") * sample_rows
    rows = first + jnp.arange(sample_rows, dtype=jnp.int32)
    own_live, other_live = rows < live[0], rows < live[1]
    blocks = held_block(jnp.arange(WHOLE_BLOCKS, dtype=jnp.int32), core)

    layers = jnp.concatenate([maps, lax.ppermute(maps, AXES, LAYERS)]).reshape(-1, sample_rows)
    wanted = lax.dynamic_index_in_dim(jnp.asarray(MAP_ROWS), me, 0, keepdims=False)
    targets = jnp.take(layers, wanted, axis=0)
    x, y, z, owner = coordinates(targets >> 7)
    grid = lax.axis_index("grid")
    mine = (grid & 3, (grid >> 2) & 3, (grid >> 4) * 2 + (lax.axis_index("front") >> 1))
    ours = functools.reduce(
        jnp.logical_and,
        [(((v - 1 + core) & 3) >> 1) == (((m - 1 + core) & 3) >> 1) for v, m in zip((x, y, z), mine)],
    )
    member = sum(((((v - core) & 3) >> 1) << i) for i, v in enumerate((x, y, z)))
    slots = jnp.where(ours, (member * 2 + (owner ^ core)) * own_rows + (targets & (own_rows - 1)), -1)
    own_slots, other_slots = slots[0::2].reshape(-1), slots[1::2].reshape(-1)

    near, other_update, own_at, other_at, own_live, other_live, blocks, own_slots, other_slots = lax.optimization_barrier(
        (near, other_update, own_at, other_at, own_live, other_live, blocks, own_slots, other_slots)
    )
    gathered = spread(near.reshape(-1, width), FAR).reshape(-1, width)
    gathered, given_front = lax.optimization_barrier((gathered, own_front))
    other_front = swap_cores(given_front)

    def masked(sample, alive):
        return jnp.where(alive[:, None], sample, jnp.float32(0.0))

    own_sample = child_product(own_at, gathered, own_update, SMALL_LIMIT)
    own_cube = spread(masked(own_sample, own_live), NEAR).reshape(-1, width)
    _, other_at = lax.optimization_barrier((own_sample, other_at))
    other_sample = child_product(other_at, gathered, other_update, VMEM_LIMIT)
    other_cube = spread(masked(other_sample, other_live), NEAR).reshape(-1, width)
    own_cube, _, blocks = lax.optimization_barrier((own_cube, other_sample, blocks))
    front = front_product(blocks, gathered, own_front, other_front)

    def placed(cube, at_slots):
        chosen = (jnp.arange(16 * own_rows, dtype=jnp.int32)[:, None] == at_slots[None, :]).astype(jnp.bfloat16)
        terms = jnp.dot(chosen, jnp.concatenate(halves(cube), axis=1), preferred_element_type=jnp.float32)
        return terms[:, :width] + terms[:, width:]

    own_terms = placed(own_cube, own_slots)
    _, other_cube, front = lax.optimization_barrier((own_terms, other_cube, front))
    terms = own_terms + placed(other_cube, other_slots)
    parts = lax.all_to_all(terms.reshape(8, 2 * own_rows, width), AXES, 0, 0, tiled=True, axis_index_groups=FAR)
    total = front + jnp.sum(parts, axis=0)
    mine_half, other_half = total[:own_rows], swap_cores(total[own_rows:])
    return jnp.where(
        core == 0,
        jnp.concatenate([mine_half, other_half], axis=1),
        jnp.concatenate([other_half, mine_half], axis=1),
    )


VMEM_LIMIT = 48 << 20
SMALL_LIMIT = 32 << 20
WHOLE_BLOCKS = len(PLACES)


def solution(mesh):
    placed = (
        P("front", None),
        P("front"),
        P("front", "grid", None),
        P(("front", "grid"), None),
        P(("front", "grid"), None),
    )
    return jax.shard_map(
        shards, mesh=mesh, in_specs=placed, out_specs=P(("front", "grid"), None), check_vma=False
    )
```

time: 177 us -> 175 us (0.989)
  waiting for transfers between devices: 67.4 us -> 15.2 us
  blocking collectives: 18 us -> 62.7 us
  starting transfers between devices: 24.2 us -> 39.1 us
  local copies, waits for them, and re-layouts: 12.9 us -> 6.69 us
  Pallas kernels: 40.9 us -> 37.5 us
    all_to_all x2 -> x3, waiting for transfers between devices: 58.9 us -> 6.16 us  [spread(): lax.all_to_all(copies, AXES, 0, 0, tiled=True, axis_index_groups=groups)]
    all_to_all x1, blocking collectives: 18 us -> 51.3 us  [spread(): lax.all_to_all(copies, AXES, 0, 0, tiled=True, axis_index_groups=groups)]
    all_to_all x2 -> x3, starting transfers between devices: 14.9 us -> 26.7 us  [spread(): lax.all_to_all(copies, AXES, 0, 0, tiled=True, axis_index_groups=groups)]
    all_to_all x0 -> x1, blocking collectives: none -> 11.4 us  [shards(): lax.all_to_all(terms.reshape(8, 2 * own_rows, width), AXES, 0, 0, tiled=T...]
    unnamed x7 -> x8, local copies, waits for them, and re-layouts: 6.77 us -> 0.03 us
    ppermute x5, waiting for transfers between devices: 2.39 us -> 9.08 us  [swap_cores(): return lax.ppermute(a, AXES, CORES)]
    ppermute x1, waiting for transfers between devices: 6.13 us -> 0.01 us  [shards(): lax.ppermute(maps, AXES, LAYERS)]
    ppermute x5, starting transfers between devices: 4.51 us -> 10.6 us  [swap_cores(): return lax.ppermute(a, AXES, CORES)]
  transfers between devices with their start and end apart: 9 -> 9, of which waited for: 6 -> 3; matrix products, arithmetic and copies ran while one was open for 9% -> 8% of each run, Pallas kernels for 23% -> 22%
where the time goes in v2:
time: 175 us; the launch traced here: 174 us
  blocking collectives  62.7 us (36%)
  starting transfers between devices  39.1 us (22%)
  Pallas kernels  37.5 us (21%)
  waiting for transfers between devices  15.2 us (9%)
  local copies, waits for them, and re-layouts  6.69 us (4%)
  matrix products  6.42 us (4%)
  other arithmetic  5.81 us (3%)
    all_to_all x1, blocking collectives, spread(): lax.all_to_all(copies, AXES, 0, 0, tiled=True, axis_index_groups=groups)  51.3 us
    all_to_all x3, starting transfers between devices, spread(): lax.all_to_all(copies, AXES, 0, 0, tiled=True, axis_index_groups=groups)  26.7 us
    pallas_call x2, Pallas kernels, child_product(): pl.pallas_call(functools.partial(child_kernel, depth), out_shape=jax.Shap...  24.2 us
    pallas_call x1, Pallas kernels, front_product(): pl.pallas_call(functools.partial(front_kernel, depth), out_shape=jax.Shap...  13.4 us
    all_to_all x1, blocking collectives, shards(): lax.all_to_all(terms.reshape(8, 2 * own_rows, width), AXES, 0, 0, tiled=T...  11.4 us
    ppermute x5, starting transfers between devices, swap_cores(): return lax.ppermute(a, AXES, CORES)  10.6 us
    ppermute x5, waiting for transfers between devices, swap_cores(): return lax.ppermute(a, AXES, CORES)  9.08 us
    dot_general x2, matrix products, placed(): jnp.dot(chosen, jnp.concatenate(halves(cube), axis=1), preferred_element_...  6.42 us
  transfers between devices with their start and end apart: 9, of which 3 were waited for; matrix products, arithmetic and copies ran while one was open for 8% of the time, Pallas kernels for 22%

profile of v2, /device:TPU:1, one launch (start us, length us, event | category | flops | bytes accessed | tf_op | source)
XLA Modules:
  0.0 174.4 jit_solution(4100144216280805752)
XLA Ops:
  0.0 1.4 collective-permute-start.1
  2.1 0.8 concatenate.22
  2.8 0.0 collective-permute-start.2
  2.8 0.9 slice_select_fusion.1
  3.7 0.6 collective-permute-start
  4.3 0.7 fusion.33
  5.0 0.7 compare_and_fusion
  5.8 0.6 slice.71
  6.4 7.8 %collective-permute-done.2 = s32[8320]{0:T(1024)S(1)} collective-permute-done((s32[8320]{0:T(1024)S(1)}, s32[8320]{0:T(1024)S(1)}, u32[]{:S(2)}, u32[]{:S(2)}) %collective-permute-start.2) | collective-permute-done | bytes 33312 | tf_op jit(solution)/shard_map/ppermute | solution.py:80
  14.3 0.6 slice.72
  14.9 0.4 and_add_fusion
  15.2 1.8 %collective-permute-start.3 = (s32[2,8192]{1,0:T(2,128)S(1)}, s32[2,8192]{1,0:T(2,128)S(1)}, u32[]{:S(2)}, u32[]{:S(2)}) collective-permute-start(s32[2,8192]{1,0:T(2,128)S(1)} %get-tuple-element.38), channel_id=1, source_target_pairs={{0,64},{1,65},{2,66},{3,67},{4,68},{5,69},{6,70},{7,71},{8,72},{9,... | collective-permute-start | bytes 196616 | tf_op jit(solution)/shard_map/ppermute | solution.py:245
  17.0 0.1 fusion.37
  17.1 1.3 fusion.15
  18.4 0.0 collective-permute-done
  18.5 1.1 broadcast_in_dim.66
  19.6 10.4 %all-to-all-start = ((f32[8,256,128]{2,1,0:T(8,128)}), f32[8,256,128]{2,1,0:T(8,128)S(1)}, u32[]{:S(2)}, u32[]{:S(2)}) async-start(f32[8,256,128]{2,1,0:T(8,128)} %broadcast_in_dim.66), calls=%async_computation | async-start | bytes 2097152 | tf_op jit(solution)/shard_map/all_to_all | solution.py:85
  30.0 0.0 collective-permute-done.3
  30.0 0.1 pad_add_fusion
  30.1 0.1 reshape.67
  30.2 0.6 gather_fusion
  30.7 0.1 add_select_fusion
  30.9 6.2 %all-to-all-done = f32[8,256,128]{2,1,0:T(8,128)S(1)} async-done(((f32[8,256,128]{2,1,0:T(8,128)}), f32[8,256,128]{2,1,0:T(8,128)S(1)}, u32[]{:S(2)}, u32[]{:S(2)}) %all-to-all-start) | async-done | bytes 1048608 | tf_op jit(solution)/shard_map/all_to_all | solution.py:85
  37.1 0.0 collective-permute-done.1.update
  37.1 0.0 slice-start
  37.1 0.5 broadcast_in_dim.72
  37.6 0.0 slice-start.1
  37.6 51.3 %all_to_all.25 = f32[8,2048,128]{2,1,0:T(8,128)S(1)} all-to-all(f32[8,2048,128]{2,1,0:T(8,128)S(1)} %broadcast_in_dim.72), channel_id=1, replica_groups={{69,70,73,74,21,22,25,26},{68,71,72,75,20,23,24,27},{65,66,77,78,17,18,..., dimensions={0} | all-to-all | bytes 16777216 | tf_op jit(solution)/shard_map/all_to_all | solution.py:85
  88.9 0.0 copy-start
  88.9 8.5 %collective-permute-start.4 = (f32[128,16384]{1,0:T(8,128)}, f32[128,16384]{1,0:T(8,128)}, u32[]{:S(2)}, u32[]{:S(2)}) collective-permute-start(f32[128,16384]{1,0:T(8,128)} %own.1), channel_id=1, source_target_pairs={{0,32},{1,33},{2,34},{3,35},{4,36},{5,37},{6,38},{7,39},{8,40},{9,... | collective-permute-start | bytes 25165832 | tf_op jit(solution)/shard_map/ppermute | solution.py:80
  97.4 0.0 slice-done
  97.4 0.0 slice-done.1
  97.4 9.4 %child.2 = f32[256,128]{1,0:T(8,128)S(1)} custom-call(s32[8192]{0:T(1024)S(1)} %bitcast.31, f32[16384,128]{1,0:T(8,128)S(1)} %bitcast.23, f32[256,8192]{1,0:T(8,128)S(1)} %bitcast.29), custom_call_target="tpu_custom_call" | custom-call | flops 2147483648 | bytes 16777216 | tf_op jit(solution)/shard_map/child/pallas_call | solution.py:157
  106.8 0.0 copy-done
  106.8 0.1 broadcast_select_fusion.1
  106.9 1.1 broadcast_in_dim.74
  108.0 8.2 %all-to-all-start.2 = ((f32[8,256,128]{2,1,0:T(8,128)}), f32[8,256,128]{2,1,0:T(8,128)S(1)}, u32[]{:S(2)}, u32[]{:S(2)}) async-start(f32[8,256,128]{2,1,0:T(8,128)} %broadcast_in_dim.74), calls=%async_computation.2 | async-start | bytes 2097152 | tf_op jit(solution)/shard_map/all_to_all | solution.py:85
  116.2 14.8 %child.3 = f32[256,128]{1,0:T(8,128)S(1)} custom-call(s32[8192]{0:T(1024)S(1)} %bitcast.30, f32[16384,128]{1,0:T(8,128)} %bitcast.24, f32[256,8192]{1,0:T(8,128)} %collective-permute-done.1.update), custom_call_target="tpu_custom_call" | custom-call | flops 2147483648 | bytes 16777216 | tf_op jit(solution)/shard_map/child/pallas_call | solution.py:157
  131.0 0.1 broadcast_select_fusion
  131.1 0.0 all-to-all-done.2
  131.2 1.1 broadcast_in_dim.76
  132.2 8.2 %all-to-all-start.3 = ((f32[8,256,128]{2,1,0:T(8,128)}), f32[8,256,128]{2,1,0:T(8,128)S(1)}, u32[]{:S(2)}, u32[]{:S(2)}) async-start(f32[8,256,128]{2,1,0:T(8,128)} %broadcast_in_dim.76), calls=%async_computation.3 | async-start | bytes 2097152 | tf_op jit(solution)/shard_map/all_to_all | solution.py:85
  140.4 0.2 reduce-precision_convert_fusion.1
  140.5 3.2 %fusion = f32[2048,256]{1,0:T(8,128)S(1)} fusion(s32[2048]{0:T(1024)S(1)} %bitcast.40, bf16[2048,128]{1,0:T(8,128)(2,1)S(1)} %get-tuple-element.42, bf16[2048,128]{1,0:T(8,128)(2,1)S(1)} %get-tuple-element.41), kind=kOutput, calls=%fused_computation.3 | convolution fusion | flops 2153775104 | bytes 3153920 | tf_op jit(solution)/shard_map/dot_general | solution.py:279
  143.8 0.0 collective-permute-done.4.other
  143.8 13.4 %front.1 = f32[256,128]{1,0:T(8,128)S(1)} custom-call(s32[128]{0:T(128)S(1)} %fusion.24.blocks, f32[16384,128]{1,0:T(8,128)} %bitcast.25, f32[128,16384]{1,0:T(8,128)} %own.1, f32[128,16384]{1,0:T(8,128)} %collective-permute-done.4.other), custom_call_target="tpu_custom_call" | custom-call | flops 4294967296 | bytes 25165824 | tf_op jit(solution)/shard_map/front/pallas_call | solution.py:192
  157.1 0.0 all-to-all-done.3
  157.1 0.2 reduce-precision_convert_fusion
  157.3 3.2 %fusion.1 = f32[2048,256]{1,0:T(8,128)S(1)} fusion(s32[2048]{0:T(1024)S(1)} %bitcast.39, bf16[2048,128]{1,0:T(8,128)(2,1)S(1)} %get-tuple-element.40, bf16[2048,128]{1,0:T(8,128)(2,1)S(1)} %get-tuple-element.39), kind=kOutput, calls=%fused_computation.4 | convolution fusion | flops 2153775104 | bytes 3153920 | tf_op jit(solution)/shard_map/dot_general | solution.py:279
  160.5 0.4 fusion.6
  160.9 11.4 %all_to_all.26 = f32[8,256,128]{2,1,0:T(8,128)S(1)} all-to-all(f32[8,256,128]{2,1,0:T(8,128)S(1)} %bitcast.33), channel_id=1, replica_groups={{69,70,73,74,21,22,25,26},{68,71,72,75,20,23,24,27},{65,66,77,78,17,18,..., dimensions={0} | all-to-all | bytes 2097152 | tf_op jit(solution)/shard_map/all_to_all | solution.py:285
  172.3 0.1 reduce_sum.9
  172.4 0.1 collective-permute-start.5
  172.5 1.2 collective-permute-done.5
  173.7 0.7 maximum_select_fusion
  (12 shorter events, 0.2 us)
Async XLA Ops:
  0.0 37.1 %collective-permute-start.1 = (f32[256,8192]{1,0:T(8,128)}, f32[256,8192]{1,0:T(8,128)}, u32[]{:S(2)}, u32[]{:S(2)}) collective-permute-start(f32[256,8192]{1,0:T(8,128)} %bitcast.26), channel_id=1, source_target_pairs={{0,32},{1,33},{2,34},{3,35},{4,36},{5,37},{6,38},{7,39},{8,40},{9,... | collective-permute-start | bytes 25165832 | tf_op jit(solution)/shard_map/ppermute | solution.py:80
  2.8 11.4 %collective-permute-start.2 = (s32[8320]{0:T(1024)S(1)}, s32[8320]{0:T(1024)S(1)}, u32[]{:S(2)}, u32[]{:S(2)}) collective-permute-start(s32[8320]{0:T(1024)S(1)} %concatenate.22), channel_id=1, source_target_pairs={{0,32},{1,33},{2,34},{3,35},{4,36},{5,37},{6,38},{7,39},{8,40},{9,... | collective-permute-start | bytes 99848 | tf_op jit(solution)/shard_map/ppermute | solution.py:80
  3.7 14.7 %collective-permute-start = (f32[128,128]{1,0:T(8,128)S(1)}, f32[128,128]{1,0:T(8,128)S(1)}, u32[]{:S(2)}, u32[]{:S(2)}) collective-permute-start(f32[128,128]{1,0:T(8,128)S(1)} %get-tuple-element.46), channel_id=1, source_target_pairs={{0,32},{1,33},{2,34},{3,35},{4,36},{5,37},{6,38},{7,39},{8,40},{9,... | collective-permute-start | bytes 196616 | tf_op jit(solution)/shard_map/ppermute | solution.py:80
  15.2 14.7 %collective-permute-start.3 = (s32[2,8192]{1,0:T(2,128)S(1)}, s32[2,8192]{1,0:T(2,128)S(1)}, u32[]{:S(2)}, u32[]{:S(2)}) collective-permute-start(s32[2,8192]{1,0:T(2,128)S(1)} %get-tuple-element.38), channel_id=1, source_target_pairs={{0,64},{1,65},{2,66},{3,67},{4,68},{5,69},{6,70},{7,71},{8,72},{9,... | collective-permute-start | bytes 196616 | tf_op jit(solution)/shard_map/ppermute | solution.py:245
  19.6 17.4 %all-to-all-start = ((f32[8,256,128]{2,1,0:T(8,128)}), f32[8,256,128]{2,1,0:T(8,128)S(1)}, u32[]{:S(2)}, u32[]{:S(2)}) async-start(f32[8,256,128]{2,1,0:T(8,128)} %broadcast_in_dim.66), calls=%async_computation | async-start | bytes 2097152 | tf_op jit(solution)/shard_map/all_to_all | solution.py:85
  37.1 60.3 %slice-start = ((s8[8388608]{0:T(1024)(128)(4,1)}), s8[4194304]{0:T(1024)(128)(4,1)S(1)}, s32[]{:S(2)}) async-start(s8[8388608]{0:T(1024)(128)(4,1)} %bitcast.27), calls=%async_computation.5 | async-start | bytes 8388608
  37.6 59.8 %slice-start.1 = ((s8[8388608]{0:T(1024)(128)(4,1)}), s8[4194304]{0:T(1024)(128)(4,1)S(1)}, s32[]{:S(2)}) async-start(s8[8388608]{0:T(1024)(128)(4,1)} %bitcast.27), calls=%async_computation.6 | async-start | bytes 8388608
  88.9 17.9 %copy-start = (f32[8,2048,128]{2,1,0:T(8,128)}, f32[8,2048,128]{2,1,0:T(8,128)S(1)}, u32[]{:S(2)}) copy-start(f32[8,2048,128]{2,1,0:T(8,128)S(1)} %all_to_all.25) | copy-start | bytes 25165828
  88.9 54.9 %collective-permute-start.4 = (f32[128,16384]{1,0:T(8,128)}, f32[128,16384]{1,0:T(8,128)}, u32[]{:S(2)}, u32[]{:S(2)}) collective-permute-start(f32[128,16384]{1,0:T(8,128)} %own.1), channel_id=1, source_target_pairs={{0,32},{1,33},{2,34},{3,35},{4,36},{5,37},{6,38},{7,39},{8,40},{9,... | collective-permute-start | bytes 25165832 | tf_op jit(solution)/shard_map/ppermute | solution.py:80
  108.0 23.1 %all-to-all-start.2 = ((f32[8,256,128]{2,1,0:T(8,128)}), f32[8,256,128]{2,1,0:T(8,128)S(1)}, u32[]{:S(2)}, u32[]{:S(2)}) async-start(f32[8,256,128]{2,1,0:T(8,128)} %broadcast_in_dim.74), calls=%async_computation.2 | async-start | bytes 2097152 | tf_op jit(solution)/shard_map/all_to_all | solution.py:85
  132.2 24.9 %all-to-all-start.3 = ((f32[8,256,128]{2,1,0:T(8,128)}), f32[8,256,128]{2,1,0:T(8,128)S(1)}, u32[]{:S(2)}, u32[]{:S(2)}) async-start(f32[8,256,128]{2,1,0:T(8,128)} %broadcast_in_dim.76), calls=%async_computation.3 | async-start | bytes 2097152 | tf_op jit(solution)/shard_map/all_to_all | solution.py:85
  172.4 1.3 collective-permute-start.5

commit v3 on v2

--- a/solution.py
+++ b/solution.py
@@ -58,6 +58,7 @@
 NEAR = near_groups()
 FAR = far_groups()
 CORES = [(i, DEVICE[(x, y, z, 1 - core)]) for i, (x, y, z, core) in enumerate(PLACES)]
+BOTH = [(i, DEVICE[(x, y, z ^ 1, 1 - core)]) for i, (x, y, z, core) in enumerate(PLACES)]
 LAYERS = [(i, DEVICE[(x, y, z ^ 1, core)]) for i, (x, y, z, core) in enumerate(PLACES)]
 
 
@@ -101,15 +102,15 @@
     return (p[:m, :n] + p[m:, :n]) + (p[:m, n:] + p[m:, n:])
 
 
-def child_kernel(depth, at, random, update, out, even, odd, fetched, sems):
-    chunks = update.shape[1] // depth
+def child_kernel(depth, own_at, other_at, random, own, other, own_out, other_out, even, odd, own_held, other_held, sems):
+    chunks = own.shape[1] // depth
     place = lax.broadcasted_iota(jnp.int32, (8, 128), 0)
 
-    def fetch(chunk, slot):
+    def fetch(chunk, update, held, sem):
         columns = pl.ds(pl.multiple_of(chunk * depth, depth), depth)
-        return pltpu.make_async_copy(update.at[:, columns], fetched.at[slot], sems.at[slot])
-
-    def gather(chunk, rows):
+        return pltpu.make_async_copy(update.at[:, columns], held, sem)
+
+    def gather(at, chunk, rows):
         base = chunk * depth
         for j in range(0, depth, 8):
             tile = jnp.broadcast_to(random[pl.ds(at[base + j], 1), :], (8, 128))
@@ -118,57 +119,62 @@
                 tile = jnp.where(place == t, row, tile)
             rows[j : j + 8, :] = tile
 
-    def product(slot, rows):
-        stacked = jnp.concatenate(held_halves(fetched[slot]), axis=0)
+    def product(held, rows, out):
+        stacked = jnp.concatenate(held_halves(held[...]), axis=0)
         columns = jnp.concatenate(held_halves(rows[...]), axis=1)
         out[...] += joined(jnp.dot(stacked, columns, preferred_element_type=jnp.float32))
 
-    fetch(0, 0).start()
-    fetch(1, 1).start()
-    gather(0, even)
-    out[...] = jnp.zeros_like(out)
-
-    def pair(i, carry):
-        fetch(2 * i, 0).wait()
-        gather(2 * i + 1, odd)
-        product(0, even)
-
-        @pl.when(2 * i + 2 < chunks)
+    fetch(0, own, own_held, sems.at[0]).start()
+    fetch(0, other, other_held, sems.at[1]).start()
+    gather(own_at, 0, even)
+    own_out[...] = jnp.zeros_like(own_out)
+    other_out[...] = jnp.zeros_like(other_out)
+
+    def step(i, carry):
+        fetch(i, own, own_held, sems.at[0]).wait()
+        gather(other_at, i, odd)
+        product(own_held, even, own_out)
+
+        @pl.when(i + 1 < chunks)
         def _():
-            fetch(2 * i + 2, 0).start()
-
-        fetch(2 * i + 1, 1).wait()
-        gather(jnp.minimum(2 * i + 2, chunks - 1), even)
-        product(1, odd)
-
-        @pl.when(2 * i + 3 < chunks)
+            fetch(i + 1, own, own_held, sems.at[0]).start()
+
+        fetch(i, other, other_held, sems.at[1]).wait()
+        gather(own_at, jnp.minimum(i + 1, chunks - 1), even)
+        product(other_held, odd, other_out)
+
+        @pl.when(i + 1 < chunks)
         def _():
-            fetch(2 * i + 3, 1).start()
+            fetch(i + 1, other, other_held, sems.at[1]).start()
 
         return carry
 
-    lax.fori_loop(0, chunks // 2, pair, 0)
-
-
-def child_product(at, random, update, limit, depth=1024):
-    rows, inner = update.shape
+    lax.fori_loop(0, chunks, step, 0)
+
+
+def child_products(own_at, other_at, random, own, other, depth=1024):
+    rows, inner = own.shape
     width = random.shape[1]
     whole = pl.BlockSpec(memory_space=pltpu.VMEM)
+    anywhere = pl.BlockSpec(memory_space=pl.ANY)
+    index = pl.BlockSpec(memory_space=pltpu.SMEM)
+    out = jax.ShapeDtypeStruct((rows, width), jnp.float32)
     return pl.pallas_call(
         functools.partial(child_kernel, depth),
-        out_shape=jax.ShapeDtypeStruct((rows, width), jnp.float32),
-        in_specs=[pl.BlockSpec(memory_space=pltpu.SMEM), whole, pl.BlockSpec(memory_space=pl.ANY)],
-        out_specs=whole,
+        out_shape=(out, out),
+        in_specs=[index, index, whole, anywhere, anywhere],
+        out_specs=(whole, whole),
         scratch_shapes=[
             pltpu.VMEM((depth, width), jnp.float32),
             pltpu.VMEM((depth, width), jnp.float32),
-            pltpu.VMEM((2, rows, depth), jnp.float32),
+            pltpu.VMEM((rows, depth), jnp.float32),
+            pltpu.VMEM((rows, depth), jnp.float32),
             pltpu.SemaphoreType.DMA((2,)),
         ],
-        compiler_params=pltpu.CompilerParams(vmem_limit_bytes=limit),
-        cost_estimate=pl.CostEstimate(flops=8 * rows * inner * width, bytes_accessed=16 << 20, transcendentals=0),
+        compiler_params=pltpu.CompilerParams(vmem_limit_bytes=SMALL_LIMIT),
+        cost_estimate=pl.CostEstimate(flops=16 * rows * inner * width, bytes_accessed=24 << 20, transcendentals=0),
         name="child",
-    )(at, random, update)
+    )(own_at, other_at, random, own, other)
 
 
 def front_kernel(depth, blocks, random, own, other, out):
@@ -228,21 +234,26 @@
     left, right = random[:, :width], random[:, width:]
     kept = jnp.where(core == 0, left, right)
     given = jnp.where(core == 0, right, left)
-    near = spread(jnp.concatenate([kept, swap_cores(given)], axis=0), NEAR)
-    other_update = swap_cores(own_update)
+    halved = jnp.concatenate([kept, swap_cores(given)], axis=0)
+    near = spread(halved, NEAR)
 
     own_map = jnp.concatenate([index_map[0], jnp.broadcast_to(lengths, (128,))])
-    maps = jnp.stack([own_map, swap_cores(own_map)])
-    live = maps[:, -1]
-    maps = maps[:, :-128]
+    next_maps = [lax.ppermute(own_map, AXES, pairs) for pairs in (CORES, LAYERS, BOTH)]
+    _, given_update, all_maps = lax.optimization_barrier((halved, own_update, (own_map, *next_maps)))
+    other_update = swap_cores(given_update)
+
+    all_maps = jnp.stack(all_maps)
+    live = all_maps[:2, -1]
+    all_maps = all_maps[:, :-128]
+    maps = all_maps[:2]
     at = held_block(maps >> 7, core) * 128 + (maps & 127)
     own_at, other_at = at[0], at[1]
     first = lax.axis_index("grid") * sample_rows
     rows = first + jnp.arange(sample_rows, dtype=jnp.int32)
-    own_live, other_live = rows < live[0], rows < live[1]
+    alive = rows[None, :] < live[:, None]
     blocks = held_block(jnp.arange(WHOLE_BLOCKS, dtype=jnp.int32), core)
 
-    layers = jnp.concatenate([maps, lax.ppermute(maps, AXES, LAYERS)]).reshape(-1, sample_rows)
+    layers = all_maps.reshape(-1, sample_rows)
     wanted = lax.dynamic_index_in_dim(jnp.asarray(MAP_ROWS), me, 0, keepdims=False)
     targets = jnp.take(layers, wanted, axis=0)
     x, y, z, owner = coordinates(targets >> 7)
@@ -254,34 +265,25 @@
     )
     member = sum(((((v - core) & 3) >> 1) << i) for i, v in enumerate((x, y, z)))
     slots = jnp.where(ours, (member * 2 + (owner ^ core)) * own_rows + (targets & (own_rows - 1)), -1)
-    own_slots, other_slots = slots[0::2].reshape(-1), slots[1::2].reshape(-1)
-
-    near, other_update, own_at, other_at, own_live, other_live, blocks, own_slots, other_slots = lax.optimization_barrier(
-        (near, other_update, own_at, other_at, own_live, other_live, blocks, own_slots, other_slots)
+    slots = slots.reshape(-1)
+
+    near, other_update, own_at, other_at, alive, blocks, slots = lax.optimization_barrier(
+        (near, other_update, own_at, other_at, alive, blocks, slots)
     )
     gathered = spread(near.reshape(-1, width), FAR).reshape(-1, width)
     gathered, given_front = lax.optimization_barrier((gathered, own_front))
     other_front = swap_cores(given_front)
 
-    def masked(sample, alive):
-        return jnp.where(alive[:, None], sample, jnp.float32(0.0))
-
-    own_sample = child_product(own_at, gathered, own_update, SMALL_LIMIT)
-    own_cube = spread(masked(own_sample, own_live), NEAR).reshape(-1, width)
-    _, other_at = lax.optimization_barrier((own_sample, other_at))
-    other_sample = child_product(other_at, gathered, other_update, VMEM_LIMIT)
-    other_cube = spread(masked(other_sample, other_live), NEAR).reshape(-1, width)
-    own_cube, _, blocks = lax.optimization_barrier((own_cube, other_sample, blocks))
+    samples = jnp.stack(child_products(own_at, other_at, gathered, own_update, other_update))
+    samples = jnp.where(alive[:, :, None], samples, jnp.float32(0.0))
+    cube = spread(samples, NEAR).reshape(-1, width)
+    _, blocks = lax.optimization_barrier((samples, blocks))
     front = front_product(blocks, gathered, own_front, other_front)
 
-    def placed(cube, at_slots):
-        chosen = (jnp.arange(16 * own_rows, dtype=jnp.int32)[:, None] == at_slots[None, :]).astype(jnp.bfloat16)
-        terms = jnp.dot(chosen, jnp.concatenate(halves(cube), axis=1), preferred_element_type=jnp.float32)
-        return terms[:, :width] + terms[:, width:]
-
-    own_terms = placed(own_cube, own_slots)
-    _, other_cube, front = lax.optimization_barrier((own_terms, other_cube, front))
-    terms = own_terms + placed(other_cube, other_slots)
+    cube, front = lax.optimization_barrier((cube, front))
+    chosen = (jnp.arange(16 * own_rows, dtype=jnp.int32)[:, None] == slots[None, :]).astype(jnp.bfloat16)
+    terms = jnp.dot(chosen, jnp.concatenate(halves(cube), axis=1), preferred_element_type=jnp.float32)
+    terms = terms[:, :width] + terms[:, width:]
     parts = lax.all_to_all(terms.reshape(8, 2 * own_rows, width), AXES, 0, 0, tiled=True, axis_index_groups=FAR)
     total = front + jnp.sum(parts, axis=0)
     mine_half, other_half = total[:own_rows], swap_cores(total[own_rows:])

time: 175 us -> 158 us (0.903)
  waiting for transfers between devices: 15.2 us -> 8.58 us
  Pallas kernels: 37.5 us -> 32 us
  starting transfers between devices: 39.1 us -> 37.1 us
  local copies, waits for them, and re-layouts: 6.69 us -> 4.83 us
    ppermute x5 -> x4, waiting for transfers between devices: 9.08 us -> 0.91 us  [swap_cores(): return lax.ppermute(a, AXES, CORES)]
    all_to_all x3 -> x2, starting transfers between devices: 26.7 us -> 18.7 us  [spread(): lax.all_to_all(copies, AXES, 0, 0, tiled=True, axis_index_groups=groups)]
    ppermute x5 -> x4, starting transfers between devices: 10.6 us -> 16.3 us  [swap_cores(): return lax.ppermute(a, AXES, CORES)]
    pallas_call x2 -> x1, Pallas kernels: 24.2 us -> 18.6 us  [child_products(): pl.pallas_call(functools.partial(child_kernel, depth), out_shape=(out, ou...]
    ppermute x1 -> x3, waiting for transfers between devices: 0.01 us -> 2.24 us  [shards(): lax.ppermute(own_map, AXES, pairs)]
    all_to_all x3 -> x2, waiting for transfers between devices: 6.16 us -> 5.43 us  [spread(): lax.all_to_all(copies, AXES, 0, 0, tiled=True, axis_index_groups=groups)]
    broadcast_in_dim x4 -> x3, local copies, waits for them, and re-layouts: 3.87 us -> 3.21 us  [spread(): copies = jnp.broadcast_to(a[None], (len(groups[0]), *a.shape))]
    dot_general x2 -> x1, matrix products: 6.42 us -> 6.44 us  [shards(): jnp.dot(chosen, jnp.concatenate(halves(cube), axis=1), preferred_element_...]
  transfers between devices with their start and end apart: 9 -> 9, of which waited for: 3 -> 4; matrix products, arithmetic and copies ran while one was open for 8% -> 4% of each run, Pallas kernels for 22% -> 20%
where the time goes in v3:
time: 158 us; the launch traced here: 157 us
  blocking collectives  63 us (40%)
  starting transfers between devices  37.1 us (23%)
  Pallas kernels  32 us (20%)
  waiting for transfers between devices  8.58 us (5%)
  matrix products  6.44 us (4%)
  local copies, waits for them, and re-layouts  4.83 us (3%)
  other arithmetic  4.48 us (3%)
    all_to_all x1, blocking collectives, spread(): lax.all_to_all(copies, AXES, 0, 0, tiled=True, axis_index_groups=groups)  51.3 us
    all_to_all x2, starting transfers between devices, spread(): lax.all_to_all(copies, AXES, 0, 0, tiled=True, axis_index_groups=groups)  18.7 us
    pallas_call x1, Pallas kernels, child_products(): pl.pallas_call(functools.partial(child_kernel, depth), out_shape=(out, ou...  18.6 us
    ppermute x4, starting transfers between devices, swap_cores(): return lax.ppermute(a, AXES, CORES)  16.3 us
    pallas_call x1, Pallas kernels, front_product(): pl.pallas_call(functools.partial(front_kernel, depth), out_shape=jax.Shap...  13.4 us
    all_to_all x1, blocking collectives, shards(): lax.all_to_all(terms.reshape(8, 2 * own_rows, width), AXES, 0, 0, tiled=T...  11.7 us
    dot_general x1, matrix products, shards(): jnp.dot(chosen, jnp.concatenate(halves(cube), axis=1), preferred_element_...  6.44 us
    all_to_all x2, waiting for transfers between devices, spread(): lax.all_to_all(copies, AXES, 0, 0, tiled=True, axis_index_groups=groups)  5.43 us
  transfers between devices with their start and end apart: 9, of which 4 were waited for; matrix products, arithmetic and copies ran while one was open for 4% of the time, Pallas kernels for 20%

profile of v3, /device:TPU:1, one launch (start us, length us, event | category | flops | bytes accessed | tf_op | source)
XLA Modules:
  0.0 157.2 jit_solution(10705048172749028924)
XLA Ops:
  0.0 0.9 slice_select_fusion.1
  0.9 1.5 collective-permute-start
  3.0 0.8 concatenate.22
  3.8 1.6 %collective-permute-start.3 = (s32[8320]{0:T(1024)S(1)}, s32[8320]{0:T(1024)S(1)}, u32[]{:S(2)}, u32[]{:S(2)}) collective-permute-start(s32[8320]{0:T(1024)S(1)} %concatenate.22), channel_id=1, source_target_pairs={{0,96},{1,97},{2,98},{3,99},{4,100},{5,101},{6,102},{7,103},{8,104... | collective-permute-start | bytes 99848 | tf_op jit(solution)/shard_map/ppermute | solution.py:241
  5.4 0.1 collective-permute-start.2
  5.6 0.4 collective-permute-start.1
  6.0 0.0 collective-permute-done
  6.0 1.3 collective-permute-done.3
  7.3 1.0 collective-permute-done.2
  8.2 0.0 collective-permute-done.1
  8.2 1.7 %collective-permute-start.4 = (f32[256,8192]{1,0:T(8,128)}, f32[256,8192]{1,0:T(8,128)}, u32[]{:S(2)}, u32[]{:S(2)}) collective-permute-start(f32[256,8192]{1,0:T(8,128)} %bitcast.23), channel_id=1, source_target_pairs={{0,32},{1,33},{2,34},{3,35},{4,36},{5,37},{6,38},{7,39},{8,40},{9,... | collective-permute-start | bytes 25165832 | tf_op jit(solution)/shard_map/ppermute | solution.py:81
  9.9 0.7 fusion.26
  10.6 0.7 compare_and_fusion
  11.4 1.1 broadcast_in_dim.52
  12.6 10.5 %all-to-all-start = ((f32[8,256,128]{2,1,0:T(8,128)}), f32[8,256,128]{2,1,0:T(8,128)S(1)}, u32[]{:S(2)}, u32[]{:S(2)}) async-start(f32[8,256,128]{2,1,0:T(8,128)} %broadcast_in_dim.52), calls=%async_computation | async-start | bytes 2097152 | tf_op jit(solution)/shard_map/all_to_all | solution.py:86
  23.1 0.4 and_add_fusion
  23.4 0.1 fusion.29
  23.5 0.1 pad_add_fusion
  23.6 0.1 reshape.94
  23.7 0.6 gather_fusion
  24.3 0.1 select_bitcast_fusion
  24.4 0.2 fusion.9
  24.6 0.1 broadcast_compare_fusion
  24.7 5.4 %all-to-all-done = f32[8,256,128]{2,1,0:T(8,128)S(1)} async-done(((f32[8,256,128]{2,1,0:T(8,128)}), f32[8,256,128]{2,1,0:T(8,128)S(1)}, u32[]{:S(2)}, u32[]{:S(2)}) %all-to-all-start) | async-done | bytes 1048608 | tf_op jit(solution)/shard_map/all_to_all | solution.py:86
  30.1 0.0 collective-permute-done.4.other
  30.1 0.0 slice-start
  30.1 0.5 broadcast_in_dim.58
  30.7 0.0 slice-start.1
  30.7 51.3 %all_to_all.20 = f32[8,2048,128]{2,1,0:T(8,128)S(1)} all-to-all(f32[8,2048,128]{2,1,0:T(8,128)S(1)} %broadcast_in_dim.58), channel_id=1, replica_groups={{69,70,73,74,21,22,25,26},{68,71,72,75,20,23,24,27},{65,66,77,78,17,18,..., dimensions={0} | all-to-all | bytes 16777216 | tf_op jit(solution)/shard_map/all_to_all | solution.py:86
  82.0 0.0 copy-start
  82.0 7.8 %collective-permute-start.5 = (f32[128,16384]{1,0:T(8,128)}, f32[128,16384]{1,0:T(8,128)}, u32[]{:S(2)}, u32[]{:S(2)}) collective-permute-start(f32[128,16384]{1,0:T(8,128)} %own.1), channel_id=1, source_target_pairs={{0,32},{1,33},{2,34},{3,35},{4,36},{5,37},{6,38},{7,39},{8,40},{9,... | collective-permute-start | bytes 25165832 | tf_op jit(solution)/shard_map/ppermute | solution.py:81
  89.7 0.0 slice-done
  89.7 0.0 slice-done.1
  89.7 18.6 %child.1 = (f32[256,128]{1,0:T(8,128)S(1)}, f32[256,128]{1,0:T(8,128)S(1)}) custom-call(s32[8192]{0:T(1024)S(1)} %bitcast.28, s32[8192]{0:T(1024)S(1)} %bitcast.27, f32[16384,128]{1,0:T(8,128)S(1)} %bitcast.21, f32[256,8192]{1,0:T(8,128)S(1)} %bitcast.26, f32[256,8192]{1,0:T(8,128)} %collective-permute-done.4.other), custom_call_target="tpu_custom_call" | custom-call | flops 4294967296 | bytes 25165824 | tf_op jit(solution)/shard_map/child/pallas_call | solution.py:162
  108.3 0.0 copy-done
  108.3 0.1 maximum_select_fusion
  108.5 1.5 broadcast_in_dim.60
  110.0 8.2 %all-to-all-start.2 = ((f32[8,2,256,128]{3,2,1,0:T(8,128)}), f32[8,2,256,128]{3,2,1,0:T(8,128)S(1)}, u32[]{:S(2)}, u32[]{:S(2)}) async-start(f32[8,2,256,128]{3,2,1,0:T(8,128)} %broadcast_in_dim.60), calls=%async_computation.2 | async-start | bytes 4194304 | tf_op jit(solution)/shard_map/all_to_all | solution.py:86
  118.2 0.0 collective-permute-done.5.other
  118.2 13.4 %front.1 = f32[256,128]{1,0:T(8,128)S(1)} custom-call(s32[128]{0:T(128)S(1)} %fusion.17.blocks, f32[16384,128]{1,0:T(8,128)} %bitcast.22, f32[128,16384]{1,0:T(8,128)} %own.1, f32[128,16384]{1,0:T(8,128)} %collective-permute-done.5.other), custom_call_target="tpu_custom_call" | custom-call | flops 4294967296 | bytes 25165824 | tf_op jit(solution)/shard_map/front/pallas_call | solution.py:198
  131.6 0.0 all-to-all-done.2
  131.6 0.3 reduce-precision_convert_fusion
  131.9 6.4 %fusion = f32[2048,256]{1,0:T(8,128)S(1)} fusion(s32[4096]{0:T(1024)S(1)} %bitcast.35, bf16[4096,128]{1,0:T(8,128)(2,1)S(1)} %get-tuple-element.42, bf16[4096,128]{1,0:T(8,128)(2,1)S(1)} %get-tuple-element.41), kind=kOutput, calls=%fused_computation.2 | convolution fusion | flops 4307550208 | bytes 4210688 | tf_op jit(solution)/shard_map/dot_general | solution.py:285
  138.4 0.1 slice_add_fusion
  138.5 11.7 %all_to_all.21 = f32[8,256,128]{2,1,0:T(8,128)S(1)} all-to-all(f32[8,256,128]{2,1,0:T(8,128)S(1)} %bitcast.33), channel_id=1, replica_groups={{69,70,73,74,21,22,25,26},{68,71,72,75,20,23,24,27},{65,66,77,78,17,18,..., dimensions={0} | all-to-all | bytes 2097152 | tf_op jit(solution)/shard_map/all_to_all | solution.py:287
  150.2 0.1 reduce_sum.9
  150.3 5.4 %collective-permute-start.6 = (f32[128,128]{1,0:T(8,128)S(1)}, f32[128,128]{1,0:T(8,128)S(1)}, u32[]{:S(2)}, u32[]{:S(2)}) collective-permute-start(f32[128,128]{1,0:T(8,128)S(1)} %get-tuple-element.44), channel_id=1, source_target_pairs={{0,32},{1,33},{2,34},{3,35},{4,36},{5,37},{6,38},{7,39},{8,40},{9,... | collective-permute-start | bytes 196616 | tf_op jit(solution)/shard_map/ppermute | solution.py:81
  155.7 0.9 collective-permute-done.6
  156.6 0.7 maximum_select_fusion.1
  (12 shorter events, 0.2 us)
Async XLA Ops:
  0.9 5.1 %collective-permute-start = (f32[128,128]{1,0:T(8,128)S(1)}, f32[128,128]{1,0:T(8,128)S(1)}, u32[]{:S(2)}, u32[]{:S(2)}) collective-permute-start(f32[128,128]{1,0:T(8,128)S(1)} %get-tuple-element.46), channel_id=1, source_target_pairs={{0,32},{1,33},{2,34},{3,35},{4,36},{5,37},{6,38},{7,39},{8,40},{9,... | collective-permute-start | bytes 196616 | tf_op jit(solution)/shard_map/ppermute | solution.py:81
  3.8 3.5 %collective-permute-start.3 = (s32[8320]{0:T(1024)S(1)}, s32[8320]{0:T(1024)S(1)}, u32[]{:S(2)}, u32[]{:S(2)}) collective-permute-start(s32[8320]{0:T(1024)S(1)} %concatenate.22), channel_id=1, source_target_pairs={{0,96},{1,97},{2,98},{3,99},{4,100},{5,101},{6,102},{7,103},{8,104... | collective-permute-start | bytes 99848 | tf_op jit(solution)/shard_map/ppermute | solution.py:241
  5.4 2.8 %collective-permute-start.2 = (s32[8320]{0:T(1024)S(1)}, s32[8320]{0:T(1024)S(1)}, u32[]{:S(2)}, u32[]{:S(2)}) collective-permute-start(s32[8320]{0:T(1024)S(1)} %concatenate.22), channel_id=1, source_target_pairs={{0,64},{1,65},{2,66},{3,67},{4,68},{5,69},{6,70},{7,71},{8,72},{9,... | collective-permute-start | bytes 99848 | tf_op jit(solution)/shard_map/ppermute | solution.py:241
  5.6 2.7 %collective-permute-start.1 = (s32[8320]{0:T(1024)S(1)}, s32[8320]{0:T(1024)S(1)}, u32[]{:S(2)}, u32[]{:S(2)}) collective-permute-start(s32[8320]{0:T(1024)S(1)} %concatenate.22), channel_id=1, source_target_pairs={{0,32},{1,33},{2,34},{3,35},{4,36},{5,37},{6,38},{7,39},{8,40},{9,... | collective-permute-start | bytes 99848 | tf_op jit(solution)/shard_map/ppermute | solution.py:241
  8.2 21.9 %collective-permute-start.4 = (f32[256,8192]{1,0:T(8,128)}, f32[256,8192]{1,0:T(8,128)}, u32[]{:S(2)}, u32[]{:S(2)}) collective-permute-start(f32[256,8192]{1,0:T(8,128)} %bitcast.23), channel_id=1, source_target_pairs={{0,32},{1,33},{2,34},{3,35},{4,36},{5,37},{6,38},{7,39},{8,40},{9,... | collective-permute-start | bytes 25165832 | tf_op jit(solution)/shard_map/ppermute | solution.py:81
  12.6 17.5 %all-to-all-start = ((f32[8,256,128]{2,1,0:T(8,128)}), f32[8,256,128]{2,1,0:T(8,128)S(1)}, u32[]{:S(2)}, u32[]{:S(2)}) async-start(f32[8,256,128]{2,1,0:T(8,128)} %broadcast_in_dim.52), calls=%async_computation | async-start | bytes 2097152 | tf_op jit(solution)/shard_map/all_to_all | solution.py:86
  30.1 59.6 %slice-start = ((s8[8388608]{0:T(1024)(128)(4,1)}), s8[4194304]{0:T(1024)(128)(4,1)S(1)}, s32[]{:S(2)}) async-start(s8[8388608]{0:T(1024)(128)(4,1)} %bitcast.24), calls=%async_computation.4 | async-start | bytes 8388608
  30.7 59.0 %slice-start.1 = ((s8[8388608]{0:T(1024)(128)(4,1)}), s8[4194304]{0:T(1024)(128)(4,1)S(1)}, s32[]{:S(2)}) async-start(s8[8388608]{0:T(1024)(128)(4,1)} %bitcast.24), calls=%async_computation.5 | async-start | bytes 8388608
  82.0 26.4 %copy-start = (f32[8,2048,128]{2,1,0:T(8,128)}, f32[8,2048,128]{2,1,0:T(8,128)S(1)}, u32[]{:S(2)}) copy-start(f32[8,2048,128]{2,1,0:T(8,128)S(1)} %all_to_all.20) | copy-start | bytes 25165828
  82.0 36.2 %collective-permute-start.5 = (f32[128,16384]{1,0:T(8,128)}, f32[128,16384]{1,0:T(8,128)}, u32[]{:S(2)}, u32[]{:S(2)}) collective-permute-start(f32[128,16384]{1,0:T(8,128)} %own.1), channel_id=1, source_target_pairs={{0,32},{1,33},{2,34},{3,35},{4,36},{5,37},{6,38},{7,39},{8,40},{9,... | collective-permute-start | bytes 25165832 | tf_op jit(solution)/shard_map/ppermute | solution.py:81
  110.0 21.5 %all-to-all-start.2 = ((f32[8,2,256,128]{3,2,1,0:T(8,128)}), f32[8,2,256,128]{3,2,1,0:T(8,128)S(1)}, u32[]{:S(2)}, u32[]{:S(2)}) async-start(f32[8,2,256,128]{3,2,1,0:T(8,128)} %broadcast_in_dim.60), calls=%async_computation.2 | async-start | bytes 4194304 | tf_op jit(solution)/shard_map/all_to_all | solution.py:86
  150.3 6.3 %collective-permute-start.6 = (f32[128,128]{1,0:T(8,128)S(1)}, f32[128,128]{1,0:T(8,128)S(1)}, u32[]{:S(2)}, u32[]{:S(2)}) collective-permute-start(f32[128,128]{1,0:T(8,128)S(1)} %get-tuple-element.44), channel_id=1, source_target_pairs={{0,32},{1,33},{2,34},{3,35},{4,36},{5,37},{6,38},{7,39},{8,40},{9,... | collective-permute-start | bytes 196616 | tf_op jit(solution)/shard_map/ppermute | solution.py:81

commit v4 on v3

--- a/solution.py
+++ b/solution.py
@@ -26,10 +26,6 @@
 PLACES = places()
 DEVICE = {place: i for i, place in enumerate(PLACES)}
 BITS = [(z, y, x) for z in range(2) for y in range(2) for x in range(2)]
-
-
-def cube_of(v, shift):
-    return ((v - shift) % SIDE) // 2
 
 
 def near_groups():
@@ -49,16 +45,18 @@
     groups = []
     for core in range(2):
         for cube in BITS:
-            members = [DEVICE[tuple((2 * c + b + 1 - core) % SIDE for c, b in zip(cube[::-1], bit[::-1])) + (core,)] for bit in BITS]
-            members.sort(key=lambda d: tuple(cube_of(PLACES[d][i], core) for i in (2, 1, 0)))
-            groups.append(members)
+            groups.append(
+                [
+                    DEVICE[tuple((2 * c + b + 1 - core) % SIDE for c, b in zip(cube[::-1], bit[::-1])) + (core,)]
+                    for bit in BITS
+                ]
+            )
     return groups
 
 
 NEAR = near_groups()
 FAR = far_groups()
 CORES = [(i, DEVICE[(x, y, z, 1 - core)]) for i, (x, y, z, core) in enumerate(PLACES)]
-BOTH = [(i, DEVICE[(x, y, z ^ 1, 1 - core)]) for i, (x, y, z, core) in enumerate(PLACES)]
 LAYERS = [(i, DEVICE[(x, y, z ^ 1, core)]) for i, (x, y, z, core) in enumerate(PLACES)]
 
 
@@ -152,7 +150,7 @@
     lax.fori_loop(0, chunks, step, 0)
 
 
-def child_products(own_at, other_at, random, own, other, depth=1024):
+def child_products(own_at, other_at, random, own, other, depth=2048):
     rows, inner = own.shape
     width = random.shape[1]
     whole = pl.BlockSpec(memory_space=pltpu.VMEM)
@@ -191,7 +189,7 @@
     out[...] += joined(jnp.dot(stacked, columns, preferred_element_type=jnp.float32))
 
 
-def front_product(blocks, random, own, other, depth=2048):
+def front_product(blocks, random, own, other, depth=4096):
     rows, inner = own.shape
     width = random.shape[1]
     block = pl.BlockSpec((rows, depth), lambda k, *_: (0, k))
@@ -215,11 +213,17 @@
     return grid & 3, (grid >> 2) & 3, (grid >> 4) * 2 + (front >> 1), front & 1
 
 
-def held_block(block, core):
-    x, y, z, owner = coordinates(block)
-    x, y, z = (x - core) & 3, (y - core) & 3, (z - core) & 3
-    far = (z >> 1) * 4 + (y >> 1) * 2 + (x >> 1)
-    near = (z & 1) * 4 + (y & 1) * 2 + (x & 1)
+def far_cube(v, core):
+    return ((v - 1 + core) & 3) >> 1
+
+
+def held_block(block, here, core):
+    *there, owner = coordinates(block)
+    far = near = 0
+    for i, (v, m) in enumerate(zip(there, here)):
+        v = (v - core) & 3
+        far += ((v >> 1) ^ far_cube(m, core) ^ core) << i
+        near += (v & 1) << i
     return (far * 8 + near) * 2 + (owner ^ core)
 
 
@@ -228,6 +232,8 @@
     core = lax.axis_index("front") & 1
     width = random.shape[1] // 2
     own_rows = random.shape[0]
+    grid = lax.axis_index("grid")
+    here = (grid & 3, (grid >> 2) & 3, (grid >> 4) * 2 + (lax.axis_index("front") >> 1))
     sample_rows = update_front.shape[1]
 
     own_update, own_front = update_front[0], front_matrix
@@ -238,37 +244,22 @@
     near = spread(halved, NEAR)
 
     own_map = jnp.concatenate([index_map[0], jnp.broadcast_to(lengths, (128,))])
-    next_maps = [lax.ppermute(own_map, AXES, pairs) for pairs in (CORES, LAYERS, BOTH)]
-    _, given_update, all_maps = lax.optimization_barrier((halved, own_update, (own_map, *next_maps)))
+    other_map = swap_cores(own_map)
+    _, _, given_update = lax.optimization_barrier((halved, other_map, own_update))
     other_update = swap_cores(given_update)
 
-    all_maps = jnp.stack(all_maps)
-    live = all_maps[:2, -1]
-    all_maps = all_maps[:, :-128]
-    maps = all_maps[:2]
-    at = held_block(maps >> 7, core) * 128 + (maps & 127)
+    maps = jnp.stack([own_map, other_map])
+    live = maps[:, -1]
+    maps = maps[:, :-128]
+    at = held_block(maps >> 7, here, core) * 128 + (maps & 127)
     own_at, other_at = at[0], at[1]
-    first = lax.axis_index("grid") * sample_rows
+    first = grid * sample_rows
     rows = first + jnp.arange(sample_rows, dtype=jnp.int32)
     alive = rows[None, :] < live[:, None]
-    blocks = held_block(jnp.arange(WHOLE_BLOCKS, dtype=jnp.int32), core)
-
-    layers = all_maps.reshape(-1, sample_rows)
-    wanted = lax.dynamic_index_in_dim(jnp.asarray(MAP_ROWS), me, 0, keepdims=False)
-    targets = jnp.take(layers, wanted, axis=0)
-    x, y, z, owner = coordinates(targets >> 7)
-    grid = lax.axis_index("grid")
-    mine = (grid & 3, (grid >> 2) & 3, (grid >> 4) * 2 + (lax.axis_index("front") >> 1))
-    ours = functools.reduce(
-        jnp.logical_and,
-        [(((v - 1 + core) & 3) >> 1) == (((m - 1 + core) & 3) >> 1) for v, m in zip((x, y, z), mine)],
-    )
-    member = sum(((((v - core) & 3) >> 1) << i) for i, v in enumerate((x, y, z)))
-    slots = jnp.where(ours, (member * 2 + (owner ^ core)) * own_rows + (targets & (own_rows - 1)), -1)
-    slots = slots.reshape(-1)
-
-    near, other_update, own_at, other_at, alive, blocks, slots = lax.optimization_barrier(
-        (near, other_update, own_at, other_at, alive, blocks, slots)
+    blocks = held_block(jnp.arange(WHOLE_BLOCKS, dtype=jnp.int32), here, core)
+
+    near, other_update, own_at, other_at, alive, blocks = lax.optimization_barrier(
+        (near, other_update, own_at, other_at, alive, blocks)
     )
     gathered = spread(near.reshape(-1, width), FAR).reshape(-1, width)
     gathered, given_front = lax.optimization_barrier((gathered, own_front))
@@ -277,8 +268,17 @@
     samples = jnp.stack(child_products(own_at, other_at, gathered, own_update, other_update))
     samples = jnp.where(alive[:, :, None], samples, jnp.float32(0.0))
     cube = spread(samples, NEAR).reshape(-1, width)
-    _, blocks = lax.optimization_barrier((samples, blocks))
+    _, blocks, maps, here = lax.optimization_barrier((samples, blocks, maps, here))
     front = front_product(blocks, gathered, own_front, other_front)
+
+    layers = jnp.concatenate([maps, lax.ppermute(maps, AXES, LAYERS)]).reshape(-1, sample_rows)
+    wanted = lax.dynamic_index_in_dim(jnp.asarray(MAP_ROWS), me, 0, keepdims=False)
+    targets = layers.at[wanted].get(mode="promise_in_bounds")
+    *there, owner = coordinates(targets >> 7)
+    ours = functools.reduce(jnp.logical_and, [far_cube(v, core) == far_cube(m, core) for v, m in zip(there, here)])
+    member = sum(((v - 1 + core) & 1) << i for i, v in enumerate(there))
+    slots = jnp.where(ours, (member * 2 + (owner ^ core)) * own_rows + (targets & (own_rows - 1)), -1)
+    slots = slots.reshape(-1)
 
     cube, front = lax.optimization_barrier((cube, front))
     chosen = (jnp.arange(16 * own_rows, dtype=jnp.int32)[:, None] == slots[None, :]).astype(jnp.bfloat16)

time: 158 us -> 158 us (level)
  starting transfers between devices: 37.1 us -> 30.5 us
  waiting for transfers between devices: 8.58 us -> 15 us
  blocking collectives: 63 us -> 67.9 us
  Pallas kernels: 32 us -> 28.7 us
    ppermute x4 -> x5, starting transfers between devices: 16.3 us -> 8.34 us  [swap_cores(): return lax.ppermute(a, AXES, CORES)]
    ppermute x3 -> x1, waiting for transfers between devices: 2.24 us -> 6.12 us  [shards(): lax.ppermute(maps, AXES, LAYERS)]
    all_to_all x1, blocking collectives: 11.7 us -> 15.3 us  [shards(): lax.all_to_all(terms.reshape(8, 2 * own_rows, width), AXES, 0, 0, tiled=T...]
    all_to_all x2, starting transfers between devices: 18.7 us -> 22.1 us  [spread(): lax.all_to_all(copies, AXES, 0, 0, tiled=True, axis_index_groups=groups)]
    ppermute x3 -> x1, starting transfers between devices: 2.17 us -> 0.01 us  [shards(): lax.ppermute(maps, AXES, LAYERS)]
    pallas_call x1, Pallas kernels: 13.4 us -> 11.5 us  [front_product(): pl.pallas_call(functools.partial(front_kernel, depth), out_shape=jax.Shap...]
  transfers between devices with their start and end apart: 9 -> 8, of which waited for: 4 -> 4; matrix products, arithmetic and copies ran while one was open for 4% -> 4% of each run, Pallas kernels for 20% -> 18%
where the time goes in v4:
time: 158 us
  blocking collectives  67.9 us (43%)
  starting transfers between devices  30.5 us (19%)
  Pallas kernels  28.7 us (18%)
  waiting for transfers between devices  15 us (9%)
  matrix products  6.44 us (4%)
  local copies, waits for them, and re-layouts  4.78 us (3%)
  other arithmetic  3.71 us (2%)
    all_to_all x1, blocking collectives, spread(): lax.all_to_all(copies, AXES, 0, 0, tiled=True, axis_index_groups=groups)  52.6 us
    all_to_all x2, starting transfers between devices, spread(): lax.all_to_all(copies, AXES, 0, 0, tiled=True, axis_index_groups=groups)  22.1 us
    pallas_call x1, Pallas kernels, child_products(): pl.pallas_call(functools.partial(child_kernel, depth), out_shape=(out, ou...  17.2 us
    all_to_all x1, blocking collectives, shards(): lax.all_to_all(terms.reshape(8, 2 * own_rows, width), AXES, 0, 0, tiled=T...  15.3 us
    pallas_call x1, Pallas kernels, front_product(): pl.pallas_call(functools.partial(front_kernel, depth), out_shape=jax.Shap...  11.5 us
    ppermute x5, starting transfers between devices, swap_cores(): return lax.ppermute(a, AXES, CORES)  8.34 us
    all_to_all x2, waiting for transfers between devices, spread(): lax.all_to_all(copies, AXES, 0, 0, tiled=True, axis_index_groups=groups)  6.74 us
    dot_general x1, matrix products, shards(): jnp.dot(chosen, jnp.concatenate(halves(cube), axis=1), preferred_element_...  6.44 us
  transfers between devices with their start and end apart: 8, of which 4 were waited for; matrix products, arithmetic and copies ran while one was open for 4% of the time, Pallas kernels for 18%

profile of v4, /device:TPU:1, one launch (start us, length us, event | category | flops | bytes accessed | tf_op | source)
XLA Modules:
  0.0 157.9 jit_solution(5742817407220072495)
XLA Ops:
  0.0 0.9 slice_select_fusion.1
  0.9 1.5 collective-permute-start
  3.0 0.8 concatenate.23
  3.8 0.0 collective-permute-start.1
  3.8 0.0 collective-permute-done
  3.8 1.2 collective-permute-done.1
  5.0 0.2 collective-permute-start.2
  5.3 0.4 and_add_fusion
  5.7 1.1 broadcast_in_dim.23
  6.9 12.0 %all-to-all-start = ((f32[8,256,128]{2,1,0:T(8,128)}), f32[8,256,128]{2,1,0:T(8,128)S(1)}, u32[]{:S(2)}, u32[]{:S(2)}) async-start(f32[8,256,128]{2,1,0:T(8,128)} %broadcast_in_dim.23), calls=%async_computation | async-start | bytes 2097152 | tf_op jit(solution)/shard_map/all_to_all | solution.py:84
  18.9 0.1 fusion.16
  18.9 0.2 fusion.11
  19.1 0.1 broadcast_compare_fusion
  19.2 6.7 %all-to-all-done = f32[8,256,128]{2,1,0:T(8,128)S(1)} async-done(((f32[8,256,128]{2,1,0:T(8,128)}), f32[8,256,128]{2,1,0:T(8,128)S(1)}, u32[]{:S(2)}, u32[]{:S(2)}) %all-to-all-start) | async-done | bytes 1048608 | tf_op jit(solution)/shard_map/all_to_all | solution.py:84
  25.9 0.0 collective-permute-done.2.other
  25.9 0.0 slice-start
  25.9 0.5 broadcast_in_dim.46
  26.5 0.0 slice-start.1
  26.5 52.6 %all_to_all.20 = f32[8,2048,128]{2,1,0:T(8,128)S(1)} all-to-all(f32[8,2048,128]{2,1,0:T(8,128)S(1)} %broadcast_in_dim.46), channel_id=1, replica_groups={{69,70,73,74,21,22,25,26},{71,68,75,72,23,20,27,24},{77,78,65,66,29,30,..., dimensions={0} | all-to-all | bytes 16777216 | tf_op jit(solution)/shard_map/all_to_all | solution.py:84
  79.1 0.0 copy-start
  79.1 1.2 collective-permute-start.3
  80.3 0.0 slice-done
  80.3 0.0 slice-done.1
  80.3 17.2 %child.1 = (f32[256,128]{1,0:T(8,128)S(1)}, f32[256,128]{1,0:T(8,128)S(1)}) custom-call(s32[8192]{0:T(1024)S(1)} %bitcast.26, s32[8192]{0:T(1024)S(1)} %bitcast.25, f32[16384,128]{1,0:T(8,128)S(1)} %bitcast.19, f32[256,8192]{1,0:T(8,128)S(1)} %bitcast.24, f32[256,8192]{1,0:T(8,128)} %collective-permute-done.2.other), custom_call_target="tpu_custom_call" | custom-call | flops 4294967296 | bytes 25165824 | tf_op jit(solution)/shard_map/child/pallas_call | solution.py:160
  97.5 0.0 copy-done
  97.5 0.1 maximum_select_fusion
  97.6 1.5 broadcast_in_dim.48
  99.2 10.2 %all-to-all-start.2 = ((f32[8,2,256,128]{3,2,1,0:T(8,128)}), f32[8,2,256,128]{3,2,1,0:T(8,128)S(1)}, u32[]{:S(2)}, u32[]{:S(2)}) async-start(f32[8,2,256,128]{3,2,1,0:T(8,128)} %broadcast_in_dim.48), calls=%async_computation.2 | async-start | bytes 4194304 | tf_op jit(solution)/shard_map/all_to_all | solution.py:84
  109.3 0.7 fusion.12
  110.0 0.0 collective-permute-start.4
  110.1 6.1 %collective-permute-done.4 = s32[2,8192]{1,0:T(2,128)S(1)} collective-permute-done((s32[2,8192]{1,0:T(2,128)S(1)}, s32[2,8192]{1,0:T(2,128)S(1)}, u32[]{:S(2)}, u32[]{:S(2)}) %collective-permute-start.4) | collective-permute-done | bytes 65568 | tf_op jit(solution)/shard_map/ppermute | solution.py:274
  116.2 0.1 pad_add_fusion
  116.2 0.1 reshape.142
  116.3 0.6 gather_fusion
  117.0 0.0 collective-permute-done.3.other
  117.0 11.5 %front.1 = f32[256,128]{1,0:T(8,128)S(1)} custom-call(s32[128]{0:T(128)S(1)} %xor_add_fusion.blocks, f32[16384,128]{1,0:T(8,128)} %bitcast.20, f32[128,16384]{1,0:T(8,128)} %own.1, f32[128,16384]{1,0:T(8,128)} %collective-permute-done.3.other), custom_call_target="tpu_custom_call" | custom-call | flops 4294967296 | bytes 25165824 | tf_op jit(solution)/shard_map/front/pallas_call | solution.py:196
  128.5 0.0 all-to-all-done.2
  128.5 0.3 reduce-precision_convert_fusion
  128.8 6.4 %fusion = f32[2048,256]{1,0:T(8,128)S(1)} fusion(s32[4096]{0:T(1024)S(1)} %bitcast.33, bf16[4096,128]{1,0:T(8,128)(2,1)S(1)} %get-tuple-element.44, bf16[4096,128]{1,0:T(8,128)(2,1)S(1)} %get-tuple-element.43), kind=kOutput, calls=%fused_computation.2 | convolution fusion | flops 4307550208 | bytes 4210688 | tf_op jit(solution)/shard_map/dot_general | solution.py:285
  135.3 0.1 slice_add_fusion
  135.4 15.3 %all_to_all.21 = f32[8,256,128]{2,1,0:T(8,128)S(1)} all-to-all(f32[8,256,128]{2,1,0:T(8,128)S(1)} %bitcast.31), channel_id=1, replica_groups={{69,70,73,74,21,22,25,26},{71,68,75,72,23,20,27,24},{77,78,65,66,29,30,..., dimensions={0} | all-to-all | bytes 2097152 | tf_op jit(solution)/shard_map/all_to_all | solution.py:287
  150.7 0.1 reduce_sum.9
  150.8 5.5 %collective-permute-start.5 = (f32[128,128]{1,0:T(8,128)S(1)}, f32[128,128]{1,0:T(8,128)S(1)}, u32[]{:S(2)}, u32[]{:S(2)}) collective-permute-start(f32[128,128]{1,0:T(8,128)S(1)} %get-tuple-element.46), channel_id=1, source_target_pairs={{0,32},{1,33},{2,34},{3,35},{4,36},{5,37},{6,38},{7,39},{8,40},{9,... | collective-permute-start | bytes 196616 | tf_op jit(solution)/shard_map/ppermute | solution.py:79
  156.3 0.9 collective-permute-done.5
  157.2 0.7 maximum_select_fusion.1
  (11 shorter events, 0.2 us)
Async XLA Ops:
  0.9 2.9 %collective-permute-start = (f32[128,128]{1,0:T(8,128)S(1)}, f32[128,128]{1,0:T(8,128)S(1)}, u32[]{:S(2)}, u32[]{:S(2)}) collective-permute-start(f32[128,128]{1,0:T(8,128)S(1)} %get-tuple-element.48), channel_id=1, source_target_pairs={{0,32},{1,33},{2,34},{3,35},{4,36},{5,37},{6,38},{7,39},{8,40},{9,... | collective-permute-start | bytes 196616 | tf_op jit(solution)/shard_map/ppermute | solution.py:79
  3.8 1.2 collective-permute-start.1
  5.0 20.9 %collective-permute-start.2 = (f32[256,8192]{1,0:T(8,128)}, f32[256,8192]{1,0:T(8,128)}, u32[]{:S(2)}, u32[]{:S(2)}) collective-permute-start(f32[256,8192]{1,0:T(8,128)} %bitcast.21), channel_id=1, source_target_pairs={{0,32},{1,33},{2,34},{3,35},{4,36},{5,37},{6,38},{7,39},{8,40},{9,... | collective-permute-start | bytes 25165832 | tf_op jit(solution)/shard_map/ppermute | solution.py:79
  6.9 19.0 %all-to-all-start = ((f32[8,256,128]{2,1,0:T(8,128)}), f32[8,256,128]{2,1,0:T(8,128)S(1)}, u32[]{:S(2)}, u32[]{:S(2)}) async-start(f32[8,256,128]{2,1,0:T(8,128)} %broadcast_in_dim.23), calls=%async_computation | async-start | bytes 2097152 | tf_op jit(solution)/shard_map/all_to_all | solution.py:84
  25.9 54.4 %slice-start = ((s8[8388608]{0:T(1024)(128)(4,1)}), s8[4194304]{0:T(1024)(128)(4,1)S(1)}, s32[]{:S(2)}) async-start(s8[8388608]{0:T(1024)(128)(4,1)} %bitcast.22), calls=%async_computation.4 | async-start | bytes 8388608
  26.5 53.8 %slice-start.1 = ((s8[8388608]{0:T(1024)(128)(4,1)}), s8[4194304]{0:T(1024)(128)(4,1)S(1)}, s32[]{:S(2)}) async-start(s8[8388608]{0:T(1024)(128)(4,1)} %bitcast.22), calls=%async_computation.5 | async-start | bytes 8388608
  79.1 18.4 %copy-start = (f32[8,2048,128]{2,1,0:T(8,128)}, f32[8,2048,128]{2,1,0:T(8,128)S(1)}, u32[]{:S(2)}) copy-start(f32[8,2048,128]{2,1,0:T(8,128)S(1)} %all_to_all.20) | copy-start | bytes 25165828
  79.1 37.9 %collective-permute-start.3 = (f32[128,16384]{1,0:T(8,128)}, f32[128,16384]{1,0:T(8,128)}, u32[]{:S(2)}, u32[]{:S(2)}) collective-permute-start(f32[128,16384]{1,0:T(8,128)} %own.1), channel_id=1, source_target_pairs={{0,32},{1,33},{2,34},{3,35},{4,36},{5,37},{6,38},{7,39},{8,40},{9,... | collective-permute-start | bytes 25165832 | tf_op jit(solution)/shard_map/ppermute | solution.py:79
  99.2 29.3 %all-to-all-start.2 = ((f32[8,2,256,128]{3,2,1,0:T(8,128)}), f32[8,2,256,128]{3,2,1,0:T(8,128)S(1)}, u32[]{:S(2)}, u32[]{:S(2)}) async-start(f32[8,2,256,128]{3,2,1,0:T(8,128)} %broadcast_in_dim.48), calls=%async_computation.2 | async-start | bytes 4194304 | tf_op jit(solution)/shard_map/all_to_all | solution.py:84
  110.0 6.2 %collective-permute-start.4 = (s32[2,8192]{1,0:T(2,128)S(1)}, s32[2,8192]{1,0:T(2,128)S(1)}, u32[]{:S(2)}, u32[]{:S(2)}) collective-permute-start(s32[2,8192]{1,0:T(2,128)S(1)} %get-tuple-element.36), channel_id=1, source_target_pairs={{0,64},{1,65},{2,66},{3,67},{4,68},{5,69},{6,70},{7,71},{8,72},{9,... | collective-permute-start | bytes 196616 | tf_op jit(solution)/shard_map/ppermute | solution.py:274
  150.8 6.4 %collective-permute-start.5 = (f32[128,128]{1,0:T(8,128)S(1)}, f32[128,128]{1,0:T(8,128)S(1)}, u32[]{:S(2)}, u32[]{:S(2)}) collective-permute-start(f32[128,128]{1,0:T(8,128)S(1)} %get-tuple-element.46), channel_id=1, source_target_pairs={{0,32},{1,33},{2,34},{3,35},{4,36},{5,37},{6,38},{7,39},{8,40},{9,... | collective-permute-start | bytes 196616 | tf_op jit(solution)/shard_map/ppermute | solution.py:79

commit v5 on v4

--- a/solution.py
+++ b/solution.py
@@ -262,16 +262,18 @@
         (near, other_update, own_at, other_at, alive, blocks)
     )
     gathered = spread(near.reshape(-1, width), FAR).reshape(-1, width)
-    gathered, given_front = lax.optimization_barrier((gathered, own_front))
+    gathered, given_front, given_maps = lax.optimization_barrier((gathered, own_front, maps))
+    next_maps = lax.ppermute(given_maps, AXES, LAYERS)
     other_front = swap_cores(given_front)
 
     samples = jnp.stack(child_products(own_at, other_at, gathered, own_update, other_update))
     samples = jnp.where(alive[:, :, None], samples, jnp.float32(0.0))
+    samples, next_maps = lax.optimization_barrier((samples, next_maps))
     cube = spread(samples, NEAR).reshape(-1, width)
-    _, blocks, maps, here = lax.optimization_barrier((samples, blocks, maps, here))
+    _, blocks, maps, next_maps, here = lax.optimization_barrier((samples, blocks, maps, next_maps, here))
     front = front_product(blocks, gathered, own_front, other_front)
 
-    layers = jnp.concatenate([maps, lax.ppermute(maps, AXES, LAYERS)]).reshape(-1, sample_rows)
+    layers = jnp.concatenate([maps, next_maps]).reshape(-1, sample_rows)
     wanted = lax.dynamic_index_in_dim(jnp.asarray(MAP_ROWS), me, 0, keepdims=False)
     targets = layers.at[wanted].get(mode="promise_in_bounds")
     *there, owner = coordinates(targets >> 7)

time: 158 us -> 147 us (0.930)
  waiting for transfers between devices: 15 us -> 9.08 us
  starting transfers between devices: 30.5 us -> 27.9 us
  blocking collectives: 67.9 us -> 65.4 us
    ppermute x1, waiting for transfers between devices: 6.12 us -> 0.01 us  [shards(): next_maps = lax.ppermute(given_maps, AXES, LAYERS)]
    all_to_all x1, blocking collectives: 15.3 us -> 12.8 us  [shards(): lax.all_to_all(terms.reshape(8, 2 * own_rows, width), AXES, 0, 0, tiled=T...]
    ppermute x5, starting transfers between devices: 8.34 us -> 5.79 us  [swap_cores(): return lax.ppermute(a, AXES, CORES)]
  transfers between devices with their start and end apart: 8 -> 8, of which waited for: 4 -> 4; matrix products, arithmetic and copies ran while one was open for 4% -> 4% of each run, Pallas kernels for 18% -> 20%
where the time goes in v5:
time: 147 us
  blocking collectives  65.4 us (44%)
  Pallas kernels  28.7 us (20%)
  starting transfers between devices  27.9 us (19%)
  waiting for transfers between devices  9.08 us (6%)
  matrix products  6.44 us (4%)
  local copies, waits for them, and re-layouts  4.78 us (3%)
  other arithmetic  3.71 us (3%)
    all_to_all x1, blocking collectives, spread(): lax.all_to_all(copies, AXES, 0, 0, tiled=True, axis_index_groups=groups)  52.6 us
    all_to_all x2, starting transfers between devices, spread(): lax.all_to_all(copies, AXES, 0, 0, tiled=True, axis_index_groups=groups)  20.6 us
    pallas_call x1, Pallas kernels, child_products(): pl.pallas_call(functools.partial(child_kernel, depth), out_shape=(out, ou...  17.2 us
    all_to_all x1, blocking collectives, shards(): lax.all_to_all(terms.reshape(8, 2 * own_rows, width), AXES, 0, 0, tiled=T...  12.8 us
    pallas_call x1, Pallas kernels, front_product(): pl.pallas_call(functools.partial(front_kernel, depth), out_shape=jax.Shap...  11.5 us
    all_to_all x2, waiting for transfers between devices, spread(): lax.all_to_all(copies, AXES, 0, 0, tiled=True, axis_index_groups=groups)  6.98 us
    dot_general x1, matrix products, shards(): jnp.dot(chosen, jnp.concatenate(halves(cube), axis=1), preferred_element_...  6.44 us
    ppermute x5, starting transfers between devices, swap_cores(): return lax.ppermute(a, AXES, CORES)  5.79 us
  transfers between devices with their start and end apart: 8, of which 4 were waited for; matrix products, arithmetic and copies ran while one was open for 4% of the time, Pallas kernels for 20%

profile of v5, /device:TPU:1, one launch (start us, length us, event | category | flops | bytes accessed | tf_op | source)
XLA Modules:
  0.0 146.9 jit_solution(11528570528910110043)
XLA Ops:
  0.0 0.9 slice_select_fusion.1
  0.9 1.5 %collective-permute-start = (f32[128,128]{1,0:T(8,128)S(1)}, f32[128,128]{1,0:T(8,128)S(1)}, u32[]{:S(2)}, u32[]{:S(2)}) collective-permute-start(f32[128,128]{1,0:T(8,128)S(1)} %get-tuple-element.56), channel_id=1, source_target_pairs={{0,32},{1,33},{2,34},{3,35},{4,36},{5,37},{6,38},{7,39},{8,40},{9,... | collective-permute-start | bytes 196616 | tf_op jit(solution)/shard_map/ppermute | solution.py:79
  3.0 0.8 concatenate.19
  3.8 0.0 collective-permute-start.1
  3.8 0.0 collective-permute-done
  3.8 1.2 collective-permute-done.1
  5.0 0.2 collective-permute-start.2
  5.3 0.4 and_add_fusion
  5.7 1.1 broadcast_in_dim.23
  6.9 12.0 %all-to-all-start = ((f32[8,256,128]{2,1,0:T(8,128)}), f32[8,256,128]{2,1,0:T(8,128)S(1)}, u32[]{:S(2)}, u32[]{:S(2)}) async-start(f32[8,256,128]{2,1,0:T(8,128)} %broadcast_in_dim.23), calls=%async_computation | async-start | bytes 2097152 | tf_op jit(solution)/shard_map/all_to_all | solution.py:84
  18.9 0.1 fusion.16
  18.9 0.2 fusion.11
  19.1 0.1 broadcast_compare_fusion
  19.2 6.7 %all-to-all-done = f32[8,256,128]{2,1,0:T(8,128)S(1)} async-done(((f32[8,256,128]{2,1,0:T(8,128)}), f32[8,256,128]{2,1,0:T(8,128)S(1)}, u32[]{:S(2)}, u32[]{:S(2)}) %all-to-all-start) | async-done | bytes 1048608 | tf_op jit(solution)/shard_map/all_to_all | solution.py:84
  25.9 0.0 collective-permute-done.2.other
  25.9 0.0 slice-start
  25.9 0.5 broadcast_in_dim.46
  26.5 0.0 slice-start.1
  26.5 52.6 %all_to_all.20 = f32[8,2048,128]{2,1,0:T(8,128)S(1)} all-to-all(f32[8,2048,128]{2,1,0:T(8,128)S(1)} %broadcast_in_dim.46), channel_id=1, replica_groups={{69,70,73,74,21,22,25,26},{71,68,75,72,23,20,27,24},{77,78,65,66,29,30,..., dimensions={0} | all-to-all | bytes 16777216 | tf_op jit(solution)/shard_map/all_to_all | solution.py:84
  79.1 0.0 copy-start
  79.1 1.2 collective-permute-start.4
  80.3 1.5 %collective-permute-start.3 = (s32[2,8192]{1,0:T(2,128)S(1)}, s32[2,8192]{1,0:T(2,128)S(1)}, u32[]{:S(2)}, u32[]{:S(2)}) collective-permute-start(s32[2,8192]{1,0:T(2,128)S(1)} %get-tuple-element.43), channel_id=1, source_target_pairs={{0,64},{1,65},{2,66},{3,67},{4,68},{5,69},{6,70},{7,71},{8,72},{9,... | collective-permute-start | bytes 196616 | tf_op jit(solution)/shard_map/ppermute | solution.py:266
  81.8 0.0 slice-done
  81.8 0.0 slice-done.1
  81.8 17.2 %child.1 = (f32[256,128]{1,0:T(8,128)S(1)}, f32[256,128]{1,0:T(8,128)S(1)}) custom-call(s32[8192]{0:T(1024)S(1)} %bitcast.26, s32[8192]{0:T(1024)S(1)} %bitcast.25, f32[16384,128]{1,0:T(8,128)S(1)} %bitcast.19, f32[256,8192]{1,0:T(8,128)S(1)} %bitcast.24, f32[256,8192]{1,0:T(8,128)} %collective-permute-done.2.other), custom_call_target="tpu_custom_call" | custom-call | flops 4294967296 | bytes 25165824 | tf_op jit(solution)/shard_map/child/pallas_call | solution.py:160
  99.0 0.0 copy-done
  99.0 0.1 maximum_select_fusion
  99.1 0.0 collective-permute-done.3
  99.2 1.5 %broadcast_in_dim.48 = f32[8,2,256,128]{3,2,1,0:T(8,128)} broadcast(f32[2,256,128]{2,1,0:T(8,128)S(1)} %maximum_select_fusion), dimensions={1,2,3} | broadcast | bytes 2359296 | tf_op jit(solution)/shard_map/broadcast_in_dim | solution.py:83
  100.7 8.6 %all-to-all-start.2 = ((f32[8,2,256,128]{3,2,1,0:T(8,128)}), f32[8,2,256,128]{3,2,1,0:T(8,128)S(1)}, u32[]{:S(2)}, u32[]{:S(2)}) async-start(f32[8,2,256,128]{3,2,1,0:T(8,128)} %broadcast_in_dim.48), calls=%async_computation.2 | async-start | bytes 4194304 | tf_op jit(solution)/shard_map/all_to_all | solution.py:84
  109.3 0.7 fusion.12
  110.0 0.1 pad_add_fusion
  110.1 0.1 reshape.126
  110.2 0.6 gather_fusion
  110.9 0.0 collective-permute-done.4.other
  110.9 11.5 %front.1 = f32[256,128]{1,0:T(8,128)S(1)} custom-call(s32[128]{0:T(128)S(1)} %xor_add_fusion.blocks, f32[16384,128]{1,0:T(8,128)} %bitcast.20, f32[128,16384]{1,0:T(8,128)} %own.1, f32[128,16384]{1,0:T(8,128)} %collective-permute-done.4.other), custom_call_target="tpu_custom_call" | custom-call | flops 4294967296 | bytes 25165824 | tf_op jit(solution)/shard_map/front/pallas_call | solution.py:196
  122.4 0.2 all-to-all-done.2
  122.6 0.3 reduce-precision_convert_fusion
  122.9 6.4 %fusion = f32[2048,256]{1,0:T(8,128)S(1)} fusion(s32[4096]{0:T(1024)S(1)} %bitcast.33, bf16[4096,128]{1,0:T(8,128)(2,1)S(1)} %get-tuple-element.52, bf16[4096,128]{1,0:T(8,128)(2,1)S(1)} %get-tuple-element.51), kind=kOutput, calls=%fused_computation.2 | convolution fusion | flops 4307550208 | bytes 4210688 | tf_op jit(solution)/shard_map/dot_general | solution.py:287
  129.4 0.1 slice_add_fusion
  129.5 12.8 %all_to_all.21 = f32[8,256,128]{2,1,0:T(8,128)S(1)} all-to-all(f32[8,256,128]{2,1,0:T(8,128)S(1)} %bitcast.31), channel_id=1, replica_groups={{69,70,73,74,21,22,25,26},{71,68,75,72,23,20,27,24},{77,78,65,66,29,30,..., dimensions={0} | all-to-all | bytes 2097152 | tf_op jit(solution)/shard_map/all_to_all | solution.py:289
  142.3 0.1 reduce_sum.9
  142.4 2.9 %collective-permute-start.5 = (f32[128,128]{1,0:T(8,128)S(1)}, f32[128,128]{1,0:T(8,128)S(1)}, u32[]{:S(2)}, u32[]{:S(2)}) collective-permute-start(f32[128,128]{1,0:T(8,128)S(1)} %get-tuple-element.54), channel_id=1, source_target_pairs={{0,32},{1,33},{2,34},{3,35},{4,36},{5,37},{6,38},{7,39},{8,40},{9,... | collective-permute-start | bytes 196616 | tf_op jit(solution)/shard_map/ppermute | solution.py:79
  145.3 0.9 collective-permute-done.5
  146.2 0.7 maximum_select_fusion.1
  (11 shorter events, 0.2 us)
Async XLA Ops:
  0.9 2.9 %collective-permute-start = (f32[128,128]{1,0:T(8,128)S(1)}, f32[128,128]{1,0:T(8,128)S(1)}, u32[]{:S(2)}, u32[]{:S(2)}) collective-permute-start(f32[128,128]{1,0:T(8,128)S(1)} %get-tuple-element.56), channel_id=1, source_target_pairs={{0,32},{1,33},{2,34},{3,35},{4,36},{5,37},{6,38},{7,39},{8,40},{9,... | collective-permute-start | bytes 196616 | tf_op jit(solution)/shard_map/ppermute | solution.py:79
  3.8 1.2 collective-permute-start.1
  5.0 20.9 %collective-permute-start.2 = (f32[256,8192]{1,0:T(8,128)}, f32[256,8192]{1,0:T(8,128)}, u32[]{:S(2)}, u32[]{:S(2)}) collective-permute-start(f32[256,8192]{1,0:T(8,128)} %bitcast.21), channel_id=1, source_target_pairs={{0,32},{1,33},{2,34},{3,35},{4,36},{5,37},{6,38},{7,39},{8,40},{9,... | collective-permute-start | bytes 25165832 | tf_op jit(solution)/shard_map/ppermute | solution.py:79
  6.9 19.0 %all-to-all-start = ((f32[8,256,128]{2,1,0:T(8,128)}), f32[8,256,128]{2,1,0:T(8,128)S(1)}, u32[]{:S(2)}, u32[]{:S(2)}) async-start(f32[8,256,128]{2,1,0:T(8,128)} %broadcast_in_dim.23), calls=%async_computation | async-start | bytes 2097152 | tf_op jit(solution)/shard_map/all_to_all | solution.py:84
  25.9 55.8 %slice-start = ((s8[8388608]{0:T(1024)(128)(4,1)}), s8[4194304]{0:T(1024)(128)(4,1)S(1)}, s32[]{:S(2)}) async-start(s8[8388608]{0:T(1024)(128)(4,1)} %bitcast.22), calls=%async_computation.4 | async-start | bytes 8388608
  26.5 55.3 %slice-start.1 = ((s8[8388608]{0:T(1024)(128)(4,1)}), s8[4194304]{0:T(1024)(128)(4,1)S(1)}, s32[]{:S(2)}) async-start(s8[8388608]{0:T(1024)(128)(4,1)} %bitcast.22), calls=%async_computation.5 | async-start | bytes 8388608
  79.1 19.9 %copy-start = (f32[8,2048,128]{2,1,0:T(8,128)}, f32[8,2048,128]{2,1,0:T(8,128)S(1)}, u32[]{:S(2)}) copy-start(f32[8,2048,128]{2,1,0:T(8,128)S(1)} %all_to_all.20) | copy-start | bytes 25165828
  79.1 31.8 %collective-permute-start.4 = (f32[128,16384]{1,0:T(8,128)}, f32[128,16384]{1,0:T(8,128)}, u32[]{:S(2)}, u32[]{:S(2)}) collective-permute-start(f32[128,16384]{1,0:T(8,128)} %own.1), channel_id=1, source_target_pairs={{0,32},{1,33},{2,34},{3,35},{4,36},{5,37},{6,38},{7,39},{8,40},{9,... | collective-permute-start | bytes 25165832 | tf_op jit(solution)/shard_map/ppermute | solution.py:79
  80.3 18.9 %collective-permute-start.3 = (s32[2,8192]{1,0:T(2,128)S(1)}, s32[2,8192]{1,0:T(2,128)S(1)}, u32[]{:S(2)}, u32[]{:S(2)}) collective-permute-start(s32[2,8192]{1,0:T(2,128)S(1)} %get-tuple-element.43), channel_id=1, source_target_pairs={{0,64},{1,65},{2,66},{3,67},{4,68},{5,69},{6,70},{7,71},{8,72},{9,... | collective-permute-start | bytes 196616 | tf_op jit(solution)/shard_map/ppermute | solution.py:266
  100.7 21.9 %all-to-all-start.2 = ((f32[8,2,256,128]{3,2,1,0:T(8,128)}), f32[8,2,256,128]{3,2,1,0:T(8,128)S(1)}, u32[]{:S(2)}, u32[]{:S(2)}) async-start(f32[8,2,256,128]{3,2,1,0:T(8,128)} %broadcast_in_dim.48), calls=%async_computation.2 | async-start | bytes 4194304 | tf_op jit(solution)/shard_map/all_to_all | solution.py:84
  142.4 3.9 %collective-permute-start.5 = (f32[128,128]{1,0:T(8,128)S(1)}, f32[128,128]{1,0:T(8,128)S(1)}, u32[]{:S(2)}, u32[]{:S(2)}) collective-permute-start(f32[128,128]{1,0:T(8,128)S(1)} %get-tuple-element.54), channel_id=1, source_target_pairs={{0,32},{1,33},{2,34},{3,35},{4,36},{5,37},{6,38},{7,39},{8,40},{9,... | collective-permute-start | bytes 196616 | tf_op jit(solution)/shard_map/ppermute | solution.py:79

commit v6 on v5

--- a/solution.py
+++ b/solution.py
@@ -241,12 +241,15 @@
     kept = jnp.where(core == 0, left, right)
     given = jnp.where(core == 0, right, left)
     halved = jnp.concatenate([kept, swap_cores(given)], axis=0)
-    near = spread(halved, NEAR)
-
     own_map = jnp.concatenate([index_map[0], jnp.broadcast_to(lengths, (128,))])
     other_map = swap_cores(own_map)
-    _, _, given_update = lax.optimization_barrier((halved, other_map, own_update))
+    halved, other_map, given_update, here, grid, core, me = lax.optimization_barrier(
+        (halved, other_map, own_update, here, grid, core, me)
+    )
     other_update = swap_cores(given_update)
+    near, own_map, other_map, here, grid, core, me = lax.optimization_barrier(
+        (spread(halved, NEAR), own_map, other_map, here, grid, core, me)
+    )
 
     maps = jnp.stack([own_map, other_map])
     live = maps[:, -1]

time: 147 us -> 146 us (level)
  blocking collectives: 65.4 us -> 83.3 us
  starting transfers between devices: 27.9 us -> 16.8 us
  waiting for transfers between devices: 9.08 us -> 2.34 us
    all_to_all x1 -> x2, blocking collectives: 52.6 us -> 70.6 us  [spread(): lax.all_to_all(copies, AXES, 0, 0, tiled=True, axis_index_groups=groups)]
    all_to_all x2 -> x1, starting transfers between devices: 20.6 us -> 8.75 us  [spread(): lax.all_to_all(copies, AXES, 0, 0, tiled=True, axis_index_groups=groups)]
    all_to_all x2 -> x1, waiting for transfers between devices: 6.98 us -> 0.24 us  [spread(): lax.all_to_all(copies, AXES, 0, 0, tiled=True, axis_index_groups=groups)]
  transfers between devices with their start and end apart: 8 -> 7, of which waited for: 4 -> 3; matrix products, arithmetic and copies ran while one was open for 4% -> 3% of each run, Pallas kernels for 20% -> 20%
where the time goes in v6:
time: 146 us
  blocking collectives  83.3 us (57%)
  Pallas kernels  28.7 us (20%)
  starting transfers between devices  16.8 us (12%)
  matrix products  6.44 us (4%)
  local copies, waits for them, and re-layouts  3.71 us (3%)
  other arithmetic  3.7 us (3%)
  waiting for transfers between devices  2.34 us (2%)
    all_to_all x2, blocking collectives, spread(): lax.all_to_all(copies, AXES, 0, 0, tiled=True, axis_index_groups=groups)  70.6 us
    pallas_call x1, Pallas kernels, child_products(): pl.pallas_call(functools.partial(child_kernel, depth), out_shape=(out, ou...  17.2 us
    all_to_all x1, blocking collectives, shards(): lax.all_to_all(terms.reshape(8, 2 * own_rows, width), AXES, 0, 0, tiled=T...  12.8 us
    pallas_call x1, Pallas kernels, front_product(): pl.pallas_call(functools.partial(front_kernel, depth), out_shape=jax.Shap...  11.5 us
    all_to_all x1, starting transfers between devices, spread(): lax.all_to_all(copies, AXES, 0, 0, tiled=True, axis_index_groups=groups)  8.75 us
    ppermute x5, starting transfers between devices, swap_cores(): return lax.ppermute(a, AXES, CORES)  6.54 us
    dot_general x1, matrix products, shards(): jnp.dot(chosen, jnp.concatenate(halves(cube), axis=1), preferred_element_...  6.44 us
  transfers between devices with their start and end apart: 7, of which 3 were waited for; matrix products, arithmetic and copies ran while one was open for 3% of the time, Pallas kernels for 20%

profile of v6, /device:TPU:1, one launch (start us, length us, event | category | flops | bytes accessed | tf_op | source)
XLA Modules:
  0.0 145.8 jit_solution(13910470909752383513)
XLA Ops:
  0.0 0.9 slice_select_fusion.1
  0.9 1.5 %collective-permute-start = (f32[128,128]{1,0:T(8,128)S(1)}, f32[128,128]{1,0:T(8,128)S(1)}, u32[]{:S(2)}, u32[]{:S(2)}) collective-permute-start(f32[128,128]{1,0:T(8,128)S(1)} %get-tuple-element.90), channel_id=1, source_target_pairs={{0,32},{1,33},{2,34},{3,35},{4,36},{5,37},{6,38},{7,39},{8,40},{9,... | collective-permute-start | bytes 196616 | tf_op jit(solution)/shard_map/ppermute | solution.py:79
  3.0 0.8 concatenate.19
  3.8 0.0 collective-permute-start.1
  3.8 0.0 collective-permute-done
  3.8 1.2 collective-permute-done.1
  5.0 0.2 collective-permute-start.2
  5.2 0.1 broadcast_in_dim.24
  5.3 18.0 %all_to_all.20 = f32[8,256,128]{2,1,0:T(8,128)S(1)} all-to-all(f32[8,256,128]{2,1,0:T(8,128)S(1)} %broadcast_in_dim.24), channel_id=1, replica_groups={{0,1,4,5,64,65,68,69},{2,3,6,7,66,67,70,71},{8,9,12,13,72,73,76,77},{10..., dimensions={0} | all-to-all | bytes 2097152 | tf_op jit(solution)/shard_map/all_to_all | solution.py:84
  23.3 0.2 fusion.11
  23.5 0.1 broadcast_compare_fusion
  23.6 0.4 and_add_fusion
  24.0 0.1 fusion.16
  24.1 0.0 collective-permute-done.2.other
  24.1 0.0 slice-start
  24.1 0.5 broadcast_in_dim.46
  24.6 0.0 slice-start.1
  24.6 52.6 %all_to_all.21 = f32[8,2048,128]{2,1,0:T(8,128)S(1)} all-to-all(f32[8,2048,128]{2,1,0:T(8,128)S(1)} %broadcast_in_dim.46), channel_id=1, replica_groups={{69,70,73,74,21,22,25,26},{71,68,75,72,23,20,27,24},{77,78,65,66,29,30,..., dimensions={0} | all-to-all | bytes 16777216 | tf_op jit(solution)/shard_map/all_to_all | solution.py:84
  77.3 0.0 copy-start
  77.3 2.0 %collective-permute-start.4 = (f32[128,16384]{1,0:T(8,128)}, f32[128,16384]{1,0:T(8,128)}, u32[]{:S(2)}, u32[]{:S(2)}) collective-permute-start(f32[128,16384]{1,0:T(8,128)} %own.1), channel_id=1, source_target_pairs={{0,32},{1,33},{2,34},{3,35},{4,36},{5,37},{6,38},{7,39},{8,40},{9,... | collective-permute-start | bytes 25165832 | tf_op jit(solution)/shard_map/ppermute | solution.py:79
  79.3 1.5 %collective-permute-start.3 = (s32[2,8192]{1,0:T(2,128)S(1)}, s32[2,8192]{1,0:T(2,128)S(1)}, u32[]{:S(2)}, u32[]{:S(2)}) collective-permute-start(s32[2,8192]{1,0:T(2,128)S(1)} %get-tuple-element.76), channel_id=1, source_target_pairs={{0,64},{1,65},{2,66},{3,67},{4,68},{5,69},{6,70},{7,71},{8,72},{9,... | collective-permute-start | bytes 196616 | tf_op jit(solution)/shard_map/ppermute | solution.py:269
  80.8 0.0 slice-done
  80.8 0.0 slice-done.1
  80.8 17.2 %child.1 = (f32[256,128]{1,0:T(8,128)S(1)}, f32[256,128]{1,0:T(8,128)S(1)}) custom-call(s32[8192]{0:T(1024)S(1)} %bitcast.26, s32[8192]{0:T(1024)S(1)} %bitcast.25, f32[16384,128]{1,0:T(8,128)S(1)} %bitcast.19, f32[256,8192]{1,0:T(8,128)S(1)} %bitcast.24, f32[256,8192]{1,0:T(8,128)} %collective-permute-done.2.other), custom_call_target="tpu_custom_call" | custom-call | flops 4294967296 | bytes 25165824 | tf_op jit(solution)/shard_map/child/pallas_call | solution.py:160
  98.0 0.0 copy-done
  98.0 0.1 maximum_select_fusion
  98.1 0.0 collective-permute-done.3
  98.1 1.5 %broadcast_in_dim.48 = f32[8,2,256,128]{3,2,1,0:T(8,128)} broadcast(f32[2,256,128]{2,1,0:T(8,128)S(1)} %maximum_select_fusion), dimensions={1,2,3} | broadcast | bytes 2359296 | tf_op jit(solution)/shard_map/broadcast_in_dim | solution.py:83
  99.6 8.7 %all-to-all-start.2 = ((f32[8,2,256,128]{3,2,1,0:T(8,128)}), f32[8,2,256,128]{3,2,1,0:T(8,128)S(1)}, u32[]{:S(2)}, u32[]{:S(2)}) async-start(f32[8,2,256,128]{3,2,1,0:T(8,128)} %broadcast_in_dim.48), calls=%async_computation.2 | async-start | bytes 4194304 | tf_op jit(solution)/shard_map/all_to_all | solution.py:84
  108.4 0.7 fusion.12
  109.1 0.1 pad_add_fusion
  109.2 0.1 reshape.126
  109.3 0.6 gather_fusion
  109.9 0.0 collective-permute-done.4.other
  109.9 11.5 %front.1 = f32[256,128]{1,0:T(8,128)S(1)} custom-call(s32[128]{0:T(128)S(1)} %xor_add_fusion.blocks, f32[16384,128]{1,0:T(8,128)} %bitcast.20, f32[128,16384]{1,0:T(8,128)} %own.1, f32[128,16384]{1,0:T(8,128)} %collective-permute-done.4.other), custom_call_target="tpu_custom_call" | custom-call | flops 4294967296 | bytes 25165824 | tf_op jit(solution)/shard_map/front/pallas_call | solution.py:196
  121.4 0.2 all-to-all-done.2
  121.7 0.3 reduce-precision_convert_fusion
  122.0 6.4 %fusion = f32[2048,256]{1,0:T(8,128)S(1)} fusion(s32[4096]{0:T(1024)S(1)} %bitcast.33, bf16[4096,128]{1,0:T(8,128)(2,1)S(1)} %get-tuple-element.86, bf16[4096,128]{1,0:T(8,128)(2,1)S(1)} %get-tuple-element.85), kind=kOutput, calls=%fused_computation.2 | convolution fusion | flops 4307550208 | bytes 4210688 | tf_op jit(solution)/shard_map/dot_general | solution.py:290
  128.4 0.1 slice_add_fusion
  128.6 12.8 %all_to_all.22 = f32[8,256,128]{2,1,0:T(8,128)S(1)} all-to-all(f32[8,256,128]{2,1,0:T(8,128)S(1)} %bitcast.31), channel_id=1, replica_groups={{69,70,73,74,21,22,25,26},{71,68,75,72,23,20,27,24},{77,78,65,66,29,30,..., dimensions={0} | all-to-all | bytes 2097152 | tf_op jit(solution)/shard_map/all_to_all | solution.py:292
  141.3 0.1 reduce_sum.9
  141.4 2.9 %collective-permute-start.5 = (f32[128,128]{1,0:T(8,128)S(1)}, f32[128,128]{1,0:T(8,128)S(1)}, u32[]{:S(2)}, u32[]{:S(2)}) collective-permute-start(f32[128,128]{1,0:T(8,128)S(1)} %get-tuple-element.88), channel_id=1, source_target_pairs={{0,32},{1,33},{2,34},{3,35},{4,36},{5,37},{6,38},{7,39},{8,40},{9,... | collective-permute-start | bytes 196616 | tf_op jit(solution)/shard_map/ppermute | solution.py:79
  144.3 0.9 collective-permute-done.5
  145.2 0.7 maximum_select_fusion.1
  (11 shorter events, 0.2 us)
Async XLA Ops:
  0.9 2.9 %collective-permute-start = (f32[128,128]{1,0:T(8,128)S(1)}, f32[128,128]{1,0:T(8,128)S(1)}, u32[]{:S(2)}, u32[]{:S(2)}) collective-permute-start(f32[128,128]{1,0:T(8,128)S(1)} %get-tuple-element.90), channel_id=1, source_target_pairs={{0,32},{1,33},{2,34},{3,35},{4,36},{5,37},{6,38},{7,39},{8,40},{9,... | collective-permute-start | bytes 196616 | tf_op jit(solution)/shard_map/ppermute | solution.py:79
  3.8 1.2 collective-permute-start.1
  5.0 19.0 %collective-permute-start.2 = (f32[256,8192]{1,0:T(8,128)}, f32[256,8192]{1,0:T(8,128)}, u32[]{:S(2)}, u32[]{:S(2)}) collective-permute-start(f32[256,8192]{1,0:T(8,128)} %bitcast.21), channel_id=1, source_target_pairs={{0,32},{1,33},{2,34},{3,35},{4,36},{5,37},{6,38},{7,39},{8,40},{9,... | collective-permute-start | bytes 25165832 | tf_op jit(solution)/shard_map/ppermute | solution.py:79
  24.1 56.7 %slice-start = ((s8[8388608]{0:T(1024)(128)(4,1)}), s8[4194304]{0:T(1024)(128)(4,1)S(1)}, s32[]{:S(2)}) async-start(s8[8388608]{0:T(1024)(128)(4,1)} %bitcast.22), calls=%async_computation.4 | async-start | bytes 8388608
  24.6 56.1 %slice-start.1 = ((s8[8388608]{0:T(1024)(128)(4,1)}), s8[4194304]{0:T(1024)(128)(4,1)S(1)}, s32[]{:S(2)}) async-start(s8[8388608]{0:T(1024)(128)(4,1)} %bitcast.22), calls=%async_computation.5 | async-start | bytes 8388608
  77.3 20.7 %copy-start = (f32[8,2048,128]{2,1,0:T(8,128)}, f32[8,2048,128]{2,1,0:T(8,128)S(1)}, u32[]{:S(2)}) copy-start(f32[8,2048,128]{2,1,0:T(8,128)S(1)} %all_to_all.21) | copy-start | bytes 25165828
  77.3 32.6 %collective-permute-start.4 = (f32[128,16384]{1,0:T(8,128)}, f32[128,16384]{1,0:T(8,128)}, u32[]{:S(2)}, u32[]{:S(2)}) collective-permute-start(f32[128,16384]{1,0:T(8,128)} %own.1), channel_id=1, source_target_pairs={{0,32},{1,33},{2,34},{3,35},{4,36},{5,37},{6,38},{7,39},{8,40},{9,... | collective-permute-start | bytes 25165832 | tf_op jit(solution)/shard_map/ppermute | solution.py:79
  79.3 18.8 %collective-permute-start.3 = (s32[2,8192]{1,0:T(2,128)S(1)}, s32[2,8192]{1,0:T(2,128)S(1)}, u32[]{:S(2)}, u32[]{:S(2)}) collective-permute-start(s32[2,8192]{1,0:T(2,128)S(1)} %get-tuple-element.76), channel_id=1, source_target_pairs={{0,64},{1,65},{2,66},{3,67},{4,68},{5,69},{6,70},{7,71},{8,72},{9,... | collective-permute-start | bytes 196616 | tf_op jit(solution)/shard_map/ppermute | solution.py:269
  99.6 22.0 %all-to-all-start.2 = ((f32[8,2,256,128]{3,2,1,0:T(8,128)}), f32[8,2,256,128]{3,2,1,0:T(8,128)S(1)}, u32[]{:S(2)}, u32[]{:S(2)}) async-start(f32[8,2,256,128]{3,2,1,0:T(8,128)} %broadcast_in_dim.48), calls=%async_computation.2 | async-start | bytes 4194304 | tf_op jit(solution)/shard_map/all_to_all | solution.py:84
  141.4 3.8 %collective-permute-start.5 = (f32[128,128]{1,0:T(8,128)S(1)}, f32[128,128]{1,0:T(8,128)S(1)}, u32[]{:S(2)}, u32[]{:S(2)}) collective-permute-start(f32[128,128]{1,0:T(8,128)S(1)} %get-tuple-element.88), channel_id=1, source_target_pairs={{0,32},{1,33},{2,34},{3,35},{4,36},{5,37},{6,38},{7,39},{8,40},{9,... | collective-permute-start | bytes 196616 | tf_op jit(solution)/shard_map/ppermute | solution.py:79

commit v7 on v6

--- a/solution.py
+++ b/solution.py
@@ -132,22 +132,19 @@
         fetch(i, own, own_held, sems.at[0]).wait()
         gather(other_at, i, odd)
         product(own_held, even, own_out)
-
-        @pl.when(i + 1 < chunks)
-        def _():
-            fetch(i + 1, own, own_held, sems.at[0]).start()
-
+        fetch(i + 1, own, own_held, sems.at[0]).start()
         fetch(i, other, other_held, sems.at[1]).wait()
-        gather(own_at, jnp.minimum(i + 1, chunks - 1), even)
+        gather(own_at, i + 1, even)
         product(other_held, odd, other_out)
-
-        @pl.when(i + 1 < chunks)
-        def _():
-            fetch(i + 1, other, other_held, sems.at[1]).start()
-
+        fetch(i + 1, other, other_held, sems.at[1]).start()
         return carry
 
-    lax.fori_loop(0, chunks, step, 0)
+    lax.fori_loop(0, chunks - 1, step, 0)
+    fetch(chunks - 1, own, own_held, sems.at[0]).wait()
+    gather(other_at, chunks - 1, odd)
+    product(own_held, even, own_out)
+    fetch(chunks - 1, other, other_held, sems.at[1]).wait()
+    product(other_held, odd, other_out)
 
 
 def child_products(own_at, other_at, random, own, other, depth=2048):

time: 146 us -> 146 us (level)
  transfers between devices with their start and end apart: 7 -> 7, of which waited for: 3 -> 3; matrix products, arithmetic and copies ran while one was open for 3% -> 3% of each run, Pallas kernels for 20% -> 19%
where the time goes in v7:
time: 146 us; the launch traced here: 145 us
  blocking collectives  83.3 us (57%)
  Pallas kernels  28.1 us (19%)
  starting transfers between devices  16.8 us (12%)
  matrix products  6.44 us (4%)
  local copies, waits for them, and re-layouts  3.71 us (3%)
  other arithmetic  3.7 us (3%)
  waiting for transfers between devices  2.34 us (2%)
    all_to_all x2, blocking collectives, spread(): lax.all_to_all(copies, AXES, 0, 0, tiled=True, axis_index_groups=groups)  70.6 us
    pallas_call x1, Pallas kernels, child_products(): pl.pallas_call(functools.partial(child_kernel, depth), out_shape=(out, ou...  16.6 us
    all_to_all x1, blocking collectives, shards(): lax.all_to_all(terms.reshape(8, 2 * own_rows, width), AXES, 0, 0, tiled=T...  12.8 us
    pallas_call x1, Pallas kernels, front_product(): pl.pallas_call(functools.partial(front_kernel, depth), out_shape=jax.Shap...  11.5 us
    all_to_all x1, starting transfers between devices, spread(): lax.all_to_all(copies, AXES, 0, 0, tiled=True, axis_index_groups=groups)  8.69 us
    ppermute x5, starting transfers between devices, swap_cores(): return lax.ppermute(a, AXES, CORES)  6.61 us
    dot_general x1, matrix products, shards(): jnp.dot(chosen, jnp.concatenate(halves(cube), axis=1), preferred_element_...  6.44 us
  transfers between devices with their start and end apart: 7, of which 3 were waited for; matrix products, arithmetic and copies ran while one was open for 3% of the time, Pallas kernels for 19%

profile of v7, /device:TPU:1, one launch (start us, length us, event | category | flops | bytes accessed | tf_op | source)
XLA Modules:
  0.0 145.3 jit_solution(15174351743755130648)
XLA Ops:
  0.0 0.9 slice_select_fusion.1
  0.9 1.5 %collective-permute-start = (f32[128,128]{1,0:T(8,128)S(1)}, f32[128,128]{1,0:T(8,128)S(1)}, u32[]{:S(2)}, u32[]{:S(2)}) collective-permute-start(f32[128,128]{1,0:T(8,128)S(1)} %get-tuple-element.90), channel_id=1, source_target_pairs={{0,32},{1,33},{2,34},{3,35},{4,36},{5,37},{6,38},{7,39},{8,40},{9,... | collective-permute-start | bytes 196616 | tf_op jit(solution)/shard_map/ppermute | solution.py:79
  3.0 0.8 concatenate.19
  3.8 0.0 collective-permute-start.1
  3.8 0.0 collective-permute-done
  3.8 1.2 collective-permute-done.1
  5.0 0.2 collective-permute-start.2
  5.2 0.1 broadcast_in_dim.24
  5.3 18.0 %all_to_all.20 = f32[8,256,128]{2,1,0:T(8,128)S(1)} all-to-all(f32[8,256,128]{2,1,0:T(8,128)S(1)} %broadcast_in_dim.24), channel_id=1, replica_groups={{0,1,4,5,64,65,68,69},{2,3,6,7,66,67,70,71},{8,9,12,13,72,73,76,77},{10..., dimensions={0} | all-to-all | bytes 2097152 | tf_op jit(solution)/shard_map/all_to_all | solution.py:84
  23.3 0.2 fusion.11
  23.5 0.1 broadcast_compare_fusion
  23.6 0.4 and_add_fusion
  24.0 0.1 fusion.16
  24.1 0.0 collective-permute-done.2.other
  24.1 0.0 slice-start
  24.1 0.5 broadcast_in_dim.46
  24.6 0.0 slice-start.1
  24.6 52.6 %all_to_all.21 = f32[8,2048,128]{2,1,0:T(8,128)S(1)} all-to-all(f32[8,2048,128]{2,1,0:T(8,128)S(1)} %broadcast_in_dim.46), channel_id=1, replica_groups={{69,70,73,74,21,22,25,26},{71,68,75,72,23,20,27,24},{77,78,65,66,29,30,..., dimensions={0} | all-to-all | bytes 16777216 | tf_op jit(solution)/shard_map/all_to_all | solution.py:84
  77.3 0.0 copy-start
  77.3 2.0 %collective-permute-start.4 = (f32[128,16384]{1,0:T(8,128)}, f32[128,16384]{1,0:T(8,128)}, u32[]{:S(2)}, u32[]{:S(2)}) collective-permute-start(f32[128,16384]{1,0:T(8,128)} %own.1), channel_id=1, source_target_pairs={{0,32},{1,33},{2,34},{3,35},{4,36},{5,37},{6,38},{7,39},{8,40},{9,... | collective-permute-start | bytes 25165832 | tf_op jit(solution)/shard_map/ppermute | solution.py:79
  79.3 1.5 %collective-permute-start.3 = (s32[2,8192]{1,0:T(2,128)S(1)}, s32[2,8192]{1,0:T(2,128)S(1)}, u32[]{:S(2)}, u32[]{:S(2)}) collective-permute-start(s32[2,8192]{1,0:T(2,128)S(1)} %get-tuple-element.76), channel_id=1, source_target_pairs={{0,64},{1,65},{2,66},{3,67},{4,68},{5,69},{6,70},{7,71},{8,72},{9,... | collective-permute-start | bytes 196616 | tf_op jit(solution)/shard_map/ppermute | solution.py:266
  80.8 0.0 slice-done
  80.8 0.0 slice-done.1
  80.8 16.6 %child.1 = (f32[256,128]{1,0:T(8,128)S(1)}, f32[256,128]{1,0:T(8,128)S(1)}) custom-call(s32[8192]{0:T(1024)S(1)} %bitcast.26, s32[8192]{0:T(1024)S(1)} %bitcast.25, f32[16384,128]{1,0:T(8,128)S(1)} %bitcast.19, f32[256,8192]{1,0:T(8,128)S(1)} %bitcast.24, f32[256,8192]{1,0:T(8,128)} %collective-permute-done.2.other), custom_call_target="tpu_custom_call" | custom-call | flops 4294967296 | bytes 25165824 | tf_op jit(solution)/shard_map/child/pallas_call | solution.py:157
  97.4 0.0 copy-done
  97.4 0.1 maximum_select_fusion
  97.5 0.0 collective-permute-done.3
  97.5 1.5 %broadcast_in_dim.48 = f32[8,2,256,128]{3,2,1,0:T(8,128)} broadcast(f32[2,256,128]{2,1,0:T(8,128)S(1)} %maximum_select_fusion), dimensions={1,2,3} | broadcast | bytes 2359296 | tf_op jit(solution)/shard_map/broadcast_in_dim | solution.py:83
  99.1 8.7 %all-to-all-start.2 = ((f32[8,2,256,128]{3,2,1,0:T(8,128)}), f32[8,2,256,128]{3,2,1,0:T(8,128)S(1)}, u32[]{:S(2)}, u32[]{:S(2)}) async-start(f32[8,2,256,128]{3,2,1,0:T(8,128)} %broadcast_in_dim.48), calls=%async_computation.2 | async-start | bytes 4194304 | tf_op jit(solution)/shard_map/all_to_all | solution.py:84
  107.8 0.7 fusion.12
  108.5 0.1 pad_add_fusion
  108.5 0.1 reshape.126
  108.6 0.6 gather_fusion
  109.3 0.0 collective-permute-done.4.other
  109.3 11.5 %front.1 = f32[256,128]{1,0:T(8,128)S(1)} custom-call(s32[128]{0:T(128)S(1)} %xor_add_fusion.blocks, f32[16384,128]{1,0:T(8,128)} %bitcast.20, f32[128,16384]{1,0:T(8,128)} %own.1, f32[128,16384]{1,0:T(8,128)} %collective-permute-done.4.other), custom_call_target="tpu_custom_call" | custom-call | flops 4294967296 | bytes 25165824 | tf_op jit(solution)/shard_map/front/pallas_call | solution.py:193
  120.8 0.2 all-to-all-done.2
  121.0 0.3 reduce-precision_convert_fusion
  121.4 6.4 %fusion = f32[2048,256]{1,0:T(8,128)S(1)} fusion(s32[4096]{0:T(1024)S(1)} %bitcast.33, bf16[4096,128]{1,0:T(8,128)(2,1)S(1)} %get-tuple-element.86, bf16[4096,128]{1,0:T(8,128)(2,1)S(1)} %get-tuple-element.85), kind=kOutput, calls=%fused_computation.2 | convolution fusion | flops 4307550208 | bytes 4210688 | tf_op jit(solution)/shard_map/dot_general | solution.py:287
  127.8 0.1 slice_add_fusion
  127.9 12.8 %all_to_all.22 = f32[8,256,128]{2,1,0:T(8,128)S(1)} all-to-all(f32[8,256,128]{2,1,0:T(8,128)S(1)} %bitcast.31), channel_id=1, replica_groups={{69,70,73,74,21,22,25,26},{71,68,75,72,23,20,27,24},{77,78,65,66,29,30,..., dimensions={0} | all-to-all | bytes 2097152 | tf_op jit(solution)/shard_map/all_to_all | solution.py:289
  140.7 0.1 reduce_sum.9
  140.8 2.9 %collective-permute-start.5 = (f32[128,128]{1,0:T(8,128)S(1)}, f32[128,128]{1,0:T(8,128)S(1)}, u32[]{:S(2)}, u32[]{:S(2)}) collective-permute-start(f32[128,128]{1,0:T(8,128)S(1)} %get-tuple-element.88), channel_id=1, source_target_pairs={{0,32},{1,33},{2,34},{3,35},{4,36},{5,37},{6,38},{7,39},{8,40},{9,... | collective-permute-start | bytes 196616 | tf_op jit(solution)/shard_map/ppermute | solution.py:79
  143.7 0.9 collective-permute-done.5
  144.6 0.7 maximum_select_fusion.1
  (11 shorter events, 0.2 us)
Async XLA Ops:
  0.9 2.9 %collective-permute-start = (f32[128,128]{1,0:T(8,128)S(1)}, f32[128,128]{1,0:T(8,128)S(1)}, u32[]{:S(2)}, u32[]{:S(2)}) collective-permute-start(f32[128,128]{1,0:T(8,128)S(1)} %get-tuple-element.90), channel_id=1, source_target_pairs={{0,32},{1,33},{2,34},{3,35},{4,36},{5,37},{6,38},{7,39},{8,40},{9,... | collective-permute-start | bytes 196616 | tf_op jit(solution)/shard_map/ppermute | solution.py:79
  3.8 1.2 collective-permute-start.1
  5.0 19.0 %collective-permute-start.2 = (f32[256,8192]{1,0:T(8,128)}, f32[256,8192]{1,0:T(8,128)}, u32[]{:S(2)}, u32[]{:S(2)}) collective-permute-start(f32[256,8192]{1,0:T(8,128)} %bitcast.21), channel_id=1, source_target_pairs={{0,32},{1,33},{2,34},{3,35},{4,36},{5,37},{6,38},{7,39},{8,40},{9,... | collective-permute-start | bytes 25165832 | tf_op jit(solution)/shard_map/ppermute | solution.py:79
  24.1 56.7 %slice-start = ((s8[8388608]{0:T(1024)(128)(4,1)}), s8[4194304]{0:T(1024)(128)(4,1)S(1)}, s32[]{:S(2)}) async-start(s8[8388608]{0:T(1024)(128)(4,1)} %bitcast.22), calls=%async_computation.4 | async-start | bytes 8388608
  24.6 56.1 %slice-start.1 = ((s8[8388608]{0:T(1024)(128)(4,1)}), s8[4194304]{0:T(1024)(128)(4,1)S(1)}, s32[]{:S(2)}) async-start(s8[8388608]{0:T(1024)(128)(4,1)} %bitcast.22), calls=%async_computation.5 | async-start | bytes 8388608
  77.3 20.1 %copy-start = (f32[8,2048,128]{2,1,0:T(8,128)}, f32[8,2048,128]{2,1,0:T(8,128)S(1)}, u32[]{:S(2)}) copy-start(f32[8,2048,128]{2,1,0:T(8,128)S(1)} %all_to_all.21) | copy-start | bytes 25165828
  77.3 32.0 %collective-permute-start.4 = (f32[128,16384]{1,0:T(8,128)}, f32[128,16384]{1,0:T(8,128)}, u32[]{:S(2)}, u32[]{:S(2)}) collective-permute-start(f32[128,16384]{1,0:T(8,128)} %own.1), channel_id=1, source_target_pairs={{0,32},{1,33},{2,34},{3,35},{4,36},{5,37},{6,38},{7,39},{8,40},{9,... | collective-permute-start | bytes 25165832 | tf_op jit(solution)/shard_map/ppermute | solution.py:79
  79.3 18.3 %collective-permute-start.3 = (s32[2,8192]{1,0:T(2,128)S(1)}, s32[2,8192]{1,0:T(2,128)S(1)}, u32[]{:S(2)}, u32[]{:S(2)}) collective-permute-start(s32[2,8192]{1,0:T(2,128)S(1)} %get-tuple-element.76), channel_id=1, source_target_pairs={{0,64},{1,65},{2,66},{3,67},{4,68},{5,69},{6,70},{7,71},{8,72},{9,... | collective-permute-start | bytes 196616 | tf_op jit(solution)/shard_map/ppermute | solution.py:266
  99.1 22.0 %all-to-all-start.2 = ((f32[8,2,256,128]{3,2,1,0:T(8,128)}), f32[8,2,256,128]{3,2,1,0:T(8,128)S(1)}, u32[]{:S(2)}, u32[]{:S(2)}) async-start(f32[8,2,256,128]{3,2,1,0:T(8,128)} %broadcast_in_dim.48), calls=%async_computation.2 | async-start | bytes 4194304 | tf_op jit(solution)/shard_map/all_to_all | solution.py:84
  140.8 3.8 %collective-permute-start.5 = (f32[128,128]{1,0:T(8,128)S(1)}, f32[128,128]{1,0:T(8,128)S(1)}, u32[]{:S(2)}, u32[]{:S(2)}) collective-permute-start(f32[128,128]{1,0:T(8,128)S(1)} %get-tuple-element.88), channel_id=1, source_target_pairs={{0,32},{1,33},{2,34},{3,35},{4,36},{5,37},{6,38},{7,39},{8,40},{9,... | collective-permute-start | bytes 196616 | tf_op jit(solution)/shard_map/ppermute | solution.py:79
